TPU v7x, 32 devices: a whole 2x2x4 slice. The times are simulated.
32 devices in a mesh: shard: 8 (over z, y), ctx: 2 (over x), tensor: 2 (over core).
Axes of the slice: x: 2, y: 2, z: 4, core: 2. Of those that a mesh axis runs over, the one named last changes fastest.
Arguments:
- tokens: bfloat16 [8, 768, 1024], P('shard', 'ctx'), may hold values from -6 to 6
- condition: bfloat16 [8, 1024], P('shard'), may hold values from -6 to 6
- ada_weight: bfloat16 [1024, 6, 1024], P('shard', None, 'tensor'), may hold values from -0.1875 to 0.1875
- ada_bias: float32 [6, 1024], P(None, 'tensor'), may hold values from -4 to 4
- qkv_weight: bfloat16 [1024, 3, 1024], P('shard', None, 'tensor'), may hold values from -0.1875 to 0.1875
- qv_bias: float32 [2, 1024], P(None, 'tensor'), may hold values from -4 to 4
- output_weight: bfloat16 [1024, 1024], P('tensor', 'shard'), may hold values from -3 to 3
- output_bias: float32 [1024], replicated, may hold values from -6 to 6
- expand_weight: bfloat16 [1024, 4096], P('shard', 'tensor'), may hold values from -0.1875 to 0.1875
- expand_bias: float32 [4096], P('tensor'), may hold values from -6 to 6
- contract_weight: bfloat16 [4096, 1024], P('tensor', 'shard'), may hold values from -0.375 to 0.375
- contract_bias: float32 [1024], replicated, may hold values from -6 to 6
- cotangent: bfloat16 [8, 768, 1024], P('shard', 'ctx'), may hold values from -6 to 6
Outputs:
- block_out: float32 [8, 768, 1024], P('shard', 'ctx')
- grad_tokens: float32 [8, 768, 1024], P('shard', 'ctx')
- grad_condition: float32 [8, 1024], P('shard')
- grad_ada_weight: float32 [1024, 6, 1024], P(('shard', 'ctx'), None, 'tensor')
- grad_ada_bias: float32 [6, 1024], P(None, 'tensor')
- grad_qkv_weight: float32 [1024, 3, 1024], P(('shard', 'ctx'), None, 'tensor')
- grad_qv_bias: float32 [2, 1024], P(None, 'tensor')
- grad_output_weight: float32 [1024, 1024], P('tensor', ('shard', 'ctx'))
- grad_output_bias: float32 [1024], replicated
- grad_expand_weight: float32 [1024, 4096], P(('shard', 'ctx'), 'tensor')
- grad_expand_bias: float32 [4096], P('tensor')
- grad_contract_weight: float32 [4096, 1024], P('tensor', ('shard', 'ctx'))
- grad_contract_bias: float32 [1024], replicated
All inputs are finite; a program needn't handle non-finite values.
Results may differ from a plain program's by a relative error of at most 0.0117.
The roundings to bfloat16 on the way count: a program that leaves them out, or rounds other values in their place, can miss the bound.
Values may be sent and summed in bfloat16 or wider, within the bound.
No kernel may reach another device: no remote copies, remote signals or barrier semaphores. Data moves between devices by JAX's collectives and lax.ppermute only.
A program may use at most 128 MiB of HBM per device.

v0:
```python
import jax
import jax.numpy as jnp
from jax import lax
from jax.experimental import pallas as pl
from jax.experimental.pallas import tpu as pltpu
from jax.sharding import PartitionSpec as P

HD = 64
EPS = 1e-06
f32 = jnp.float32
bf16 = jnp.bfloat16
HIGHEST = lax.Precision.HIGHEST


def layer_norm(values):
    center = values - jnp.mean(values, axis=-1, keepdims=True)
    inverse_std = lax.rsqrt(jnp.mean(center * center, axis=-1, keepdims=True) + EPS)
    return (center * inverse_std, inverse_std)


def norm_back(normed, inverse_std, upstream):
    return (
        upstream
        - jnp.mean(upstream, axis=-1, keepdims=True)
        - normed * jnp.mean(upstream * normed, axis=-1, keepdims=True)
    ) * inverse_std


def gelu_tanh(values):
    return jax.nn.gelu(values, approximate=True)


def gelu_back(before, upstream):
    return jax.vjp(gelu_tanh, before)[1](upstream)[0]


def silu_back(before, upstream):
    return jax.vjp(jax.nn.silu, before)[1](upstream)[0]


def dot(a, b, contract, out=f32, precision=None):
    return lax.dot_general(
        a, b, ((contract[:1], contract[1:]), ((), ())), preferred_element_type=f32, precision=precision
    ).astype(out)


def _nt(a, b):
    return lax.dot_general(a, b, (((1,), (1,)), ((), ())), preferred_element_type=f32)


def _nn(a, b):
    return lax.dot_general(a, b, (((1,), (0,)), ((), ())), preferred_element_type=f32)


def _loop(rows, chunk, step):
    if rows == chunk:
        step(slice(0, rows))
        return

    def one(c, carry):
        step(pl.ds(pl.multiple_of(c * chunk, chunk), chunk))
        return carry

    lax.fori_loop(0, rows // chunk, one, 0)


def project_kernel(chunk, count, *refs):
    tok_ref, shift_ref, scale_ref, bias_ref = refs[:4]
    pieces, (low_ref, shifted_ref, weight_ref) = refs[4 : 4 + count], refs[4 + count :]
    n = weight_ref.shape[0] // count
    for p, piece in enumerate(pieces):
        weight_ref[p * n : (p + 1) * n, :] = piece[...]
    gain = 1.0 + scale_ref[...]

    def step(at):
        normed, _ = layer_norm(tok_ref[at, :].astype(f32))
        shifted = (normed * gain + shift_ref[...]).astype(bf16)
        shifted_ref[at, :] = shifted
        low_ref[at, :] = (_nn(shifted, weight_ref[...]) + bias_ref[...]).astype(bf16)

    _loop(tok_ref.shape[0], chunk, step)


def assemble_kernel(*refs):
    out_ref = refs[-1]
    n, half = refs[0].shape[0] // 2, out_ref.shape[0] // 2
    for p, ref in enumerate(refs[:-1]):
        out_ref[p * n : (p + 1) * n, :] = ref[:n, :]
        out_ref[half + p * n : half + (p + 1) * n, :] = ref[n:, :]


def assemble(pairs):
    rows, columns = pairs[0].shape
    return pl.pallas_call(
        assemble_kernel,
        out_shape=jax.ShapeDtypeStruct((rows * len(pairs), columns), bf16),
        cost_estimate=_CHEAP,
        name="assemble",
    )(*pairs)


def project(tok, shift, scale, bias, pieces):
    rows, width = tok.shape
    columns = pieces[0].shape[1]
    return pl.pallas_call(
        lambda *refs: project_kernel(_chunk(rows), len(pieces), *refs),
        out_shape=[
            jax.ShapeDtypeStruct((rows, columns), bf16),
            jax.ShapeDtypeStruct((rows, width), bf16),
            jax.ShapeDtypeStruct((width, columns), bf16),
        ],
        cost_estimate=_CHEAP,
        name="project",
    )(tok, shift, scale, bias, *pieces)


def attend_kernel(chunk, q_ref, k_ref, v_ref, out_ref, stat_ref):
    rows, lanes = out_ref.shape
    heads = [slice(h * HD, (h + 1) * HD) for h in range(lanes // HD)]
    values_t = v_ref[...].T

    def step(at):
        outs = []
        for h, lane in enumerate(heads):
            queries = q_ref[at, lane] * bf16(HD**-0.5)
            scores = _nt(k_ref[:, lane], queries)
            top = jnp.max(scores, axis=0, keepdims=True)
            logsum = top + jnp.log(jnp.sum(jnp.exp(scores - top), axis=0, keepdims=True))
            probs = jnp.exp(scores - logsum).astype(bf16)
            outs.append(_nn(values_t[lane, :], probs))
            stat_ref[h : h + 1, at] = logsum
        out_ref[at, :] = jnp.concatenate(outs, axis=0).T.astype(bf16)

    _loop(rows, chunk, step)


def attend_back_kernel(
    chunk,
    steps,
    q_ref,
    k_ref,
    v_ref,
    grad_ref,
    out_ref,
    stat_ref,
    proj_ref,
    bias_ref,
    keys_acc,
    values_acc,
):
    rows, lanes = out_ref.shape
    scale = HD**-0.5
    heads = [slice(h * HD, (h + 1) * HD) for h in range(lanes // HD)]

    def columns(part):
        if steps == 1:
            return slice(part * lanes, (part + 1) * lanes)
        return pl.ds(pl.multiple_of((part * steps + pl.program_id(0)) * lanes, lanes), lanes)

    keys_t = k_ref[...].T
    keys_acc[...] = jnp.zeros_like(keys_acc)
    values_acc[...] = jnp.zeros_like(values_acc)
    bias_ref[...] = jnp.zeros_like(bias_ref)

    def step(at):
        grad_queries, grad_keys, grad_values = [], [], []
        product = (grad_ref[at, :].astype(f32) * out_ref[at, :].astype(f32)).T
        for h, lane in enumerate(heads):
            queries, grad = q_ref[at, lane], grad_ref[at, lane]
            row_dot = jnp.sum(product[lane, :], axis=0, keepdims=True)
            probs = jnp.exp(_nt(k_ref[:, lane], queries * bf16(scale)) - stat_ref[h : h + 1, at])
            grad_scores = (probs * (_nt(v_ref[:, lane], grad) - row_dot)).astype(bf16)
            grad_values.append(_nn(probs.astype(bf16), grad))
            grad_keys.append(_nn(grad_scores, queries))
            grad_queries.append(_nn(keys_t[lane, :], grad_scores))
        values_acc[...] += jnp.concatenate(grad_values, axis=1)
        keys_acc[...] += jnp.concatenate(grad_keys, axis=1)
        got = jnp.concatenate(grad_queries, axis=0).T * scale
        bias_ref[0:1, :] += jnp.sum(got, axis=0, keepdims=True)
        proj_ref[at, columns(0)] = got.astype(bf16)

    _loop(rows, chunk, step)
    proj_ref[:, columns(1)] = (keys_acc[...] * scale).astype(bf16)
    proj_ref[:, columns(2)] = values_acc[...].astype(bf16)
    bias_ref[1:2, :] = jnp.sum(values_acc[...], axis=0, keepdims=True)


def _chunk(rows):
    return 256 if rows % 256 == 0 else rows


_CHEAP = pl.CostEstimate(flops=1000, bytes_accessed=1000, transcendentals=0)


def _parts(qkv, lanes, steps):
    if steps == 1:
        arrays = [qkv[:, j * lanes : (j + 1) * lanes] for j in range(3)]
        return arrays, [pl.BlockSpec((qkv.shape[0], lanes), lambda i: (0, 0))] * 3
    specs = [
        pl.BlockSpec((qkv.shape[0], lanes), lambda i, j=j: (0, j * steps + i)) for j in range(3)
    ]
    return [qkv] * 3, specs


def attend(qkv, lanes):
    rows, steps = qkv.shape[0], qkv.shape[1] // (3 * lanes)
    parts, specs = _parts(qkv, lanes, steps)
    return pl.pallas_call(
        lambda *refs: attend_kernel(_chunk(rows), *refs),
        grid=(steps,),
        in_specs=specs,
        out_specs=[
            pl.BlockSpec((rows, lanes), lambda i: (0, i)),
            pl.BlockSpec((8, rows), lambda i: (i, 0)),
        ],
        out_shape=[
            jax.ShapeDtypeStruct((rows, steps * lanes), bf16),
            jax.ShapeDtypeStruct((8 * steps, rows), f32),
        ],
        cost_estimate=_CHEAP,
        name="attend",
    )(*parts)


def attend_back(qkv, grad, out, stat, lanes):
    rows, steps = qkv.shape[0], qkv.shape[1] // (3 * lanes)
    parts, specs = _parts(qkv, lanes, steps)
    own = pl.BlockSpec((rows, lanes), lambda i: (0, i))
    return pl.pallas_call(
        lambda *refs: attend_back_kernel(_chunk(rows), steps, *refs),
        grid=(steps,),
        in_specs=[
            *specs, own, own, pl.BlockSpec((8, rows), lambda i: (i, 0))
        ],
        out_specs=[
            pl.BlockSpec((rows, 3 * steps * lanes), lambda i: (0, 0)),
            pl.BlockSpec((8, lanes), lambda i: (i, 0)),
        ],
        out_shape=[
            jax.ShapeDtypeStruct((rows, 3 * steps * lanes), bf16),
            jax.ShapeDtypeStruct((8 * steps, lanes), f32),
        ],
        cost_estimate=_CHEAP,
        scratch_shapes=[pltpu.VMEM((rows, lanes), f32)] * 2,
        name="attend_back",
    )(*parts, grad, out, stat)


def layer(
    tokens,
    condition,
    ada_weight,
    ada_bias,
    qkv_weight,
    qv_bias,
    output_weight,
    output_bias,
    expand_weight,
    expand_bias,
    contract_weight,
    contract_bias,
    cotangent,
):
    latents, own_rows, width = tokens.shape
    shards = lax.axis_size("shard")
    ctxs = lax.axis_size("ctx")
    tens = lax.axis_size("tensor")
    shard_at = lax.axis_index("shard")
    ctx_at = lax.axis_index("ctx")
    tensor_at = lax.axis_index("tensor")
    blk = width // shards
    share = own_rows // tens
    cols_c = qkv_weight.shape[2]
    cols = cols_c // ctxs
    hid_c = expand_weight.shape[1]
    hid = hid_c // ctxs

    bits = shards.bit_length() - 1
    assert shards == 1 << bits

    def mask_of(place):
        return sum(((place >> i) & 1) << (bits - 1 - i) for i in range(bits))

    def swap(v, mask):
        return lax.ppermute(v, "shard", [(s, s ^ mask) for s in range(shards)])

    def tie(v, *after):
        return lax.optimization_barrier((v, *after))[0]

    def from_ctx(v, k):
        return lax.ppermute(v, "ctx", [(i, (i - k) % ctxs) for i in range(ctxs)])

    def from_core(v, k):
        return lax.ppermute(v, "tensor", [(i, (i - k) % tens) for i in range(tens)])

    def gather_half(piece):
        parts = [piece]
        for p in range(1, shards // 2):
            parts.append(swap(piece, mask_of(p)))
        return parts

    def gather_direct(piece):
        n = shards // 2
        parts = [piece] * shards
        parts[n] = swap(piece, 1)
        for p in sorted(range(1, n), key=mask_of):
            parts[p] = swap(piece, mask_of(p))
            parts[n + p] = swap(parts[p], 1)
        return parts

    def gather_shards(piece, *after):
        parts = gather_half(piece)
        if after:
            parts = lax.optimization_barrier((*parts, *after))[: len(parts)]
        half = lax.optimization_barrier(jnp.concatenate(parts, axis=0))
        other = swap(half, 1)
        return lambda *late: jnp.concatenate([half, tie(other, *late) if late else other], axis=0)

    def pair_of(piece):
        return jnp.concatenate([piece, swap(piece, 1)], axis=0)

    def gather_pairs(pair, *late):
        got = [swap(pair, mask_of(p)) for p in range(1, shards // 2)]
        got = lax.optimization_barrier((*got, *late))[: len(got)]
        return assemble([pair, *got])

    def reduce_shards(low, high, *after):
        kind = high.dtype
        got = swap(high, 1)
        if after:
            got = tie(got, *after)
        n = low.shape[0] // (shards // 2)
        own = low[:n] + got[:n].astype(f32)
        sent = [
            (low[p * n : (p + 1) * n] + got[p * n : (p + 1) * n].astype(f32)).astype(kind)
            for p in range(1, shards // 2)
        ]
        pieces = []
        for p, piece in zip(range(1, shards // 2), sent):
            pieces.append(swap(piece, mask_of(p)))

        def total(*late):
            parts = lax.optimization_barrier((*pieces, *late))[: len(pieces)] if late else pieces
            return sum((v.astype(f32) for v in parts), own)

        return total

    def gather_group(v, *late):
        rows = [from_ctx(v, k) for k in range(1, ctxs)]
        rows = [v] + [tie(r, *late) if late else r for r in rows]
        rows = jnp.concatenate(rows, axis=0)
        others = [from_core(rows, k) for k in range(1, tens)]
        return jnp.concatenate([rows] + others, axis=0)

    def reduce_cores(first, rest):
        rows = ctxs * share
        total = first
        for k in range(1, tens):
            got = from_core(rest[(k - 1) * rows : k * rows], -k)
            total = total + got.astype(f32)
        return total

    def reduce_ctx(total, *late):
        own = total[:share]
        for k in range(1, ctxs):
            piece = total[k * share : (k + 1) * share].astype(bf16)
            got = from_ctx(piece, -k)
            own = own + (tie(got, *late) if late else got).astype(f32)
        return own

    rel = lax.broadcasted_iota(jnp.int32, (width, width), 1)
    row = lax.broadcasted_iota(jnp.int32, (width, width), 0)
    rel_blk = rel // blk
    rel_mask = sum(((rel_blk >> i) & 1) << (bits - 1 - i) for i in range(bits))
    rel_glob = (shard_at ^ rel_mask) * blk + rel % blk
    order = row == rel_glob
    row_glob = ((tensor_at + row // cols_c) % tens) * cols_c + row % cols_c
    col_order = row_glob == rel_glob
    order_low = order.astype(bf16)
    order_f32 = order.astype(f32)
    col_order_f32 = col_order.astype(f32)

    def to_global(v):
        a = v.astype(bf16)
        left = v - a.astype(f32)
        b = left.astype(bf16)
        c = (left - b.astype(f32)).astype(bf16)
        return dot(a, order_low, (1, 1)) + dot(b, order_low, (1, 1)) + dot(c, order_low, (1, 1))

    cond_all = gather_shards(condition)()
    squashed_all = jax.nn.silu(cond_all.astype(f32)).astype(bf16)
    squashed_rows = lax.dynamic_slice_in_dim(squashed_all, shard_at * blk, blk, 1)
    ada_flat = ada_weight.reshape(blk, 6 * cols_c)
    mod_part = dot(squashed_rows, ada_flat, (1, 0))
    half = mod_part.shape[0] // 2
    mod_sum = reduce_shards(mod_part[:half], mod_part[half:])()
    own_mod = mod_sum.reshape(latents * 6, cols_c)
    own_mod = own_mod + jnp.tile(ada_bias, (latents, 1))
    mod_cols = jnp.concatenate([own_mod] + [from_core(own_mod, k) for k in range(1, tens)], axis=1)
    modulation = dot(mod_cols, col_order_f32, (1, 0), precision=HIGHEST).reshape(latents, 6, width)

    def per_row(v, count):
        return v[:, None, :] if count is None else jnp.broadcast_to(v[:, None, :], (latents, count, width))

    def latent_rows(v, blocks):
        if latents == 1:
            return v
        return jnp.tile(jnp.repeat(v, share, axis=0), (blocks, 1))

    blocks = ctxs * tens
    rows_own = latents * share
    del per_row

    def ctx_cols(v, size, axis):
        return lax.dynamic_slice_in_dim(v, ctx_at * size, size, axis)

    lanes = min(cols, 2 * HD)
    steps = cols // lanes

    qkv_piece = ctx_cols(qkv_weight, cols, 2).reshape(blk, 3 * cols)
    out_piece = ctx_cols(output_weight, cols, 0).T
    expand_piece = ctx_cols(expand_weight, hid, 1)
    contract_piece = ctx_cols(contract_weight, hid, 0).T
    qkv_parts = gather_direct(qkv_piece)
    biases = dot(jnp.stack([output_bias, contract_bias]), order_f32, (1, 0), precision=HIGHEST)
    out_bias, con_bias = biases[0:1], biases[1:2]
    qv_own = ctx_cols(qv_bias, cols, 1)
    expand_own = ctx_cols(expand_bias, hid, 0)

    def own_rows_of(v):
        mine = lax.dynamic_slice_in_dim(v, tensor_at * share, share, 1).reshape(rows_own, width)
        return dot(mine, order_low, (1, 0), bf16)

    tok = gather_group(own_rows_of(tokens), mod_sum)
    cot_own = own_rows_of(cotangent)
    share = rows_own

    def mod_of(i, count):
        return latent_rows(modulation[:, i], count)

    stream = tok[:share].astype(f32)
    qkv_bias = jnp.concatenate([qv_own[0], jnp.zeros((cols,), f32), qv_own[1]])[None]
    contract_pair = pair_of(contract_piece)
    qkv_low, shifted_one, qkv_full = project(
        tok, modulation[:, 0], modulation[:, 1], qkv_bias, qkv_parts
    )
    cot = gather_group(cot_own, qkv_low)
    out_t = gather_shards(out_piece, qkv_low)()
    attended, stat = attend(qkv_low, lanes)
    expand_full = gather_shards(expand_piece, attended)()
    own_block = ctxs * share

    def core_product(a, b, contract):
        rest = dot(a[own_block:], b, contract, bf16)
        first = dot(a[:own_block], b, contract)
        return reduce_cores(first, rest)

    attn_core = core_product(attended, out_t, (1, 1))
    attn_share = reduce_ctx(attn_core) + out_bias
    gate_one, gate_two = mod_of(2, 1), mod_of(5, 1)
    middle_share = stream + gate_one * attn_share
    normed_two, inverse_two = layer_norm(middle_share)
    shifted_two = gather_group((normed_two * (1.0 + mod_of(4, 1)) + mod_of(3, 1)).astype(bf16))
    hidden_pre = dot(shifted_two, expand_full, (1, 0)) + expand_own
    hidden_act = gelu_tanh(hidden_pre).astype(bf16)
    contract_t = gather_pairs(contract_pair, hidden_act)

    def latent_sum(v):
        return jnp.sum(v.reshape(latents, -1, width), axis=1)

    def latent_sum_all(v):
        return jnp.sum(v.reshape(blocks, latents, -1, width), axis=(0, 2))

    def grad_high(a, g):
        return dot(a[:, width // 2 :], g, (0, 0), bf16)

    def grad_low(a, g):
        return dot(a[:, : width // 2], g, (0, 0))

    upstream_share = cot[:share].astype(f32)
    mlp_low = (cot.astype(f32) * mod_of(5, blocks)).astype(bf16)
    contract_high = grad_high(mlp_low, hidden_act)
    grad_act = dot(tie(mlp_low, contract_high), contract_t, (1, 0))
    grad_pre = gelu_back(hidden_pre, grad_act)
    bias_expand = jnp.sum(grad_pre, axis=0)
    pre_low = grad_pre.astype(bf16)
    two_core = core_product(pre_low, expand_full, (1, 1))
    grad_shifted_two = reduce_ctx(two_core)
    normed_one, inverse_one = layer_norm(tie(tok, two_core).astype(f32))
    bias_contract = jnp.sum(upstream_share * gate_two, axis=0)
    grad_scale_two = latent_sum(grad_shifted_two * normed_two)
    grad_shift_two = latent_sum(grad_shifted_two)
    middle_grad = upstream_share + norm_back(
        normed_two, inverse_two, grad_shifted_two * (1.0 + mod_of(4, 1))
    )
    grad_gate_one = latent_sum(middle_grad * attn_share)
    grad_attn = middle_grad * gate_one
    bias_output = jnp.sum(grad_attn, axis=0)
    low_share = grad_attn.astype(bf16)
    attn_low = gather_group(low_share)
    grad_attended = dot(attn_low, out_t, (1, 0), bf16)
    proj_low, bias_heads = attend_back(qkv_low, grad_attended, attended, stat, lanes)
    bias_heads = bias_heads.reshape(steps, 8, lanes)
    bias_qv = jnp.stack([bias_heads[:, 0].reshape(cols), bias_heads[:, 1].reshape(cols)])
    pre_late = tie(pre_low, two_core)
    expand_high = grad_high(shifted_two, pre_late)
    output_high = grad_high(attn_low, attended)
    mlp_core = core_product(tie(hidden_act, two_core), contract_t, (1, 1))
    owned_contract = reduce_shards(
        grad_low(mlp_low, tie(hidden_act, two_core)), contract_high, low_share
    )
    owned_expand = reduce_shards(grad_low(shifted_two, pre_late), expand_high, proj_low)
    mlp_share = reduce_ctx(mlp_core, proj_low) + con_bias
    result_share = middle_share + gate_two * mlp_share
    grad_gate_two = latent_sum(upstream_share * mlp_share)
    qkv_high = jnp.concatenate([grad_high(shifted_one, proj_low), output_high], axis=1)
    proj_late = tie(proj_low, qkv_high)
    rest_f32 = dot(proj_late[own_block:], qkv_full, (1, 1))
    rest_low = rest_f32.astype(bf16)
    first_low = dot(tie(proj_low, rest_low)[:own_block], qkv_full, (1, 1))
    first_part = jnp.concatenate([first_low, rest_f32], axis=0)
    part_scale = latent_sum_all(first_part * normed_one)
    part_shift = latent_sum_all(first_part)
    grad_shifted_one = reduce_ctx(reduce_cores(first_low, rest_low))
    grad_stream = middle_grad + norm_back(
        normed_one[:share], inverse_one[:share], grad_shifted_one * (1.0 + mod_of(1, 1))
    )

    def token_out(v):
        v = to_global(v).reshape(latents, -1, width)
        n = v.shape[1]
        out = jnp.zeros((latents, own_rows, width), f32)
        for k in range(tens):
            piece = v if k == 0 else from_core(v, k)
            out = lax.dynamic_update_slice_in_dim(out, piece, ((tensor_at + k) % tens) * n, 1)
        return out

    grad_tokens = token_out(grad_stream)

    grad_mod = jnp.stack(
        [part_shift, part_scale, grad_gate_one, grad_shift_two, grad_scale_two, grad_gate_two], axis=1
    ).reshape(latents * 6, width)
    packet = jnp.concatenate([grad_mod, bias_output[None], bias_contract[None]], axis=0)
    packet = dot(packet, col_order_f32, (1, 1), precision=HIGHEST)
    total = packet[:, :cols_c]
    qkv_grad_low = grad_low(shifted_one, tie(proj_low, packet))
    output_grad_low = grad_low(attn_low, tie(attended, proj_low))
    both_low = jnp.concatenate([qkv_grad_low, output_grad_low], axis=1)
    owned_qkv = reduce_shards(both_low, qkv_high)()
    for k in range(1, tens):
        total = total + from_core(packet[:, k * cols_c : (k + 1) * cols_c], -k)
    side = jnp.concatenate([bias_qv.reshape(-1), bias_expand])
    flat = jnp.concatenate([total.reshape(-1), side])
    summed = total
    slot = lax.broadcasted_iota(jnp.int32, (ctxs, 1), 0)
    side_all = jnp.zeros((ctxs, side.size), f32)
    n_total = total.size
    for k in range(ctxs):
        got = flat if k == 0 else from_ctx(flat, k)
        if k:
            summed = summed + got[:n_total].reshape(total.shape)
        side_all = jnp.where(slot == (ctx_at + k) % ctxs, got[n_total:], side_all)
    qv_pad = side_all[:, : 2 * cols].reshape(ctxs, 2, cols).transpose(1, 0, 2).reshape(2, cols_c)
    expand_pad = side_all[:, 2 * cols :].reshape(hid_c)
    result = token_out(tie(result_share, summed))
    message = jnp.concatenate([summed.reshape(-1), qv_pad.reshape(-1), expand_pad])[None]
    gathered = gather_shards(message)()
    n_mod = latents * 6 * cols_c
    mod_all = gathered[:, :n_mod].reshape(shards * latents, 6 * cols_c)
    sums = jnp.sum(gathered[:, n_mod:], axis=0)
    out_cols, con_cols = sums[:cols_c], sums[cols_c : 2 * cols_c]
    grad_qv_bias = sums[2 * cols_c : 4 * cols_c].reshape(2, cols_c)
    grad_expand_bias = sums[4 * cols_c :]
    grad_ada_bias = jnp.sum(mod_all, axis=0).reshape(6, cols_c)
    own_cols = blk // ctxs
    squashed_own = lax.dynamic_slice_in_dim(squashed_all, (shard_at * ctxs + ctx_at) * own_cols, own_cols, 1)
    grad_ada = dot(squashed_own.astype(f32), mod_all, (0, 0), precision=HIGHEST).reshape(own_cols, 6, cols_c)
    cond_part = dot(mod_all, ada_flat.astype(f32), (1, 1), precision=HIGHEST)
    tail = jnp.concatenate([cond_part.reshape(-1), out_cols, con_cols])
    n_cond = cond_part.size
    cond_sum = cond_part
    vectors = jnp.zeros((2, width), f32)
    for k in range(tens):
        got = tail if k == 0 else from_core(tail, k)
        if k:
            cond_sum = cond_sum + got[:n_cond].reshape(cond_part.shape)
        vectors = lax.dynamic_update_slice_in_dim(
            vectors, got[n_cond:].reshape(2, cols_c), ((tensor_at + k) % tens) * cols_c, 1
        )
    half = cond_sum.shape[0] // 2
    both = jnp.stack([cond_sum[:half], swap(cond_sum[half:], 1)], axis=1)
    both = both.reshape(shards // 2, latents, 2, blk)
    grad_squashed = jnp.zeros((latents, width), f32)
    for p in range(shards // 2):
        got = both[p] if p == 0 else swap(both[p], mask_of(p))
        for j in range(2):
            at = (shard_at ^ mask_of(p) ^ j) * blk
            grad_squashed = lax.dynamic_update_slice_in_dim(grad_squashed, got[:, j], at, 1)
    grad_cond = silu_back(condition.astype(f32), grad_squashed)

    def to_owner(v, widths):
        rows = blk // ctxs
        outs = [jnp.zeros((rows, n * ctxs), f32) for n in widths]
        for k in range(ctxs):
            piece = lax.dynamic_slice_in_dim(v, ((ctx_at - k) % ctxs) * rows, rows, 0)
            if k:
                piece = from_ctx(piece.astype(bf16), k).astype(f32)
            at = 0
            for i, n in enumerate(widths):
                outs[i] = lax.dynamic_update_slice_in_dim(
                    outs[i], piece[:, at : at + n], ((ctx_at + k) % ctxs) * n, 1
                )
                at += n
        return outs

    owned_early = jnp.concatenate([owned_expand(gathered), owned_contract(summed)], axis=1)
    grad_expand, grad_contract = to_owner(owned_early, (hid, hid))
    *grad_qkv, grad_output = to_owner(owned_qkv, (cols,) * 4)
    grad_qkv = jnp.stack(grad_qkv, axis=1)
    grad_contract, grad_output = grad_contract.T, grad_output.T
    return (
        result,
        grad_tokens,
        grad_cond,
        grad_ada,
        grad_ada_bias,
        grad_qkv,
        grad_qv_bias,
        grad_output,
        vectors[0],
        grad_expand,
        grad_expand_bias,
        grad_contract,
        vectors[1],
    )


def solution(mesh):
    in_specs = (
        P("shard", "ctx", None),
        P("shard", None),
        P("shard", None, "tensor"),
        P(None, "tensor"),
        P("shard", None, "tensor"),
        P(None, "tensor"),
        P("tensor", "shard"),
        P(),
        P("shard", "tensor"),
        P("tensor"),
        P("tensor", "shard"),
        P(),
        P("shard", "ctx", None),
    )
    out_specs = (
        P("shard", "ctx", None),
        P("shard", "ctx", None),
        P("shard", None),
        P(("shard", "ctx"), None, "tensor"),
        P(None, "tensor"),
        P(("shard", "ctx"), None, "tensor"),
        P(None, "tensor"),
        P("tensor", ("shard", "ctx")),
        P(),
        P(("shard", "ctx"), "tensor"),
        P("tensor"),
        P("tensor", ("shard", "ctx")),
        P(),
    )
    return jax.shard_map(layer, mesh=mesh, in_specs=in_specs, out_specs=out_specs, check_vma=False)
```

profile of v0, /device:TPU:0, one launch (start us, length us, event | category | flops | bytes accessed | tf_op | source)
XLA Modules:
  0.0 380.1 jit_solution(79970561516004737)
XLA Ops:
  0.7 5.1 %collective-permute-start.2 = (bf16[1,1024]{1,0:T(2,128)(2,1)}, bf16[1,1024]{1,0:T(2,128)(2,1)S(1)}, u32[]{:S(2)}, u32[]{:S(2)}) collective-permute-start(bf16[1,1024]{1,0:T(2,128)(2,1)} %param.14), channel_id=1, source_target_pairs={{0,24},{4,28},{8,16},{12,20},{16,8},{20,12},{24,0},{28,4},{1,25},{... | collective-permute-start | bytes 6152 | tf_op jit(solution)/shard_map/ppermute | solution.py:285
  8.3 1.7 collective-permute-start.9
  10.3 2.2 collective-permute-start.11
  12.6 1.6 collective-permute-start.3
  18.2 2.6 collective-permute-done.4
  23.0 2.3 collective-permute-start.5
  30.7 3.4 fusion.3
  42.9 1.9 collective-permute-done.14.refs_8_
  46.4 2.7 collective-permute-done.15.refs_9_
  49.8 3.5 collective-permute-start.20
  53.2 2.4 pad_maximum_fusion.1.refs_0_
  57.5 6.3 %project.1 = (bf16[768,768]{1,0:T(8,128)(2,1)}, bf16[768,1024]{1,0:T(8,128)(2,1)}, bf16[1024,768]{1,0:T(8,128)(2,1)}) custom-call(bf16[768,1024]{1,0:T(8,128)(2,1)} %pad_maximum_fusion.1.refs_0_, f32[1,1024]{1,0:T(1,128)} %get-tuple-element.174.refs_1_, f32[1,1024]{1,0:T(1,128)} %get-tuple-element.173.refs_2_, f32[1,768]{1,0:T(1,128)} %broadcast_in_dim.54.refs_3_, ...), custom_call_target="tpu_custom_call" | custom-call | flops 1000 | bytes 1000 | tf_op jit(solution)/shard_map/project/pallas_call | solution.py:105
  64.0 1.6 collective-permute-start.21
  65.5 11.2 %attend.1 = (bf16[768,256]{1,0:T(8,128)(2,1)}, f32[16,768]{1,0:T(8,128)}) custom-call(bf16[768,768]{1,0:T(8,128)(2,1)} %get-tuple-element.52.refs_0_.refs_1_.refs_2_, bf16[768,768]{1,0:T(8,128)(2,1)} %get-tuple-element.52.refs_0_.refs_1_.refs_2_, bf16[768,768]{1,0:T(8,128)(2,1)} %get-tuple-element.52.refs_0_.refs_1_.refs_2_), custom_call_target="tpu_custom_call" | custom-call | flops 1000 | bytes 1000 | tf_op jit(solution)/shard_map/attend/pallas_call | solution.py:208
  76.8 2.3 convolution_convert_fusion.3
  79.1 1.6 collective-permute-start.26
  80.7 2.5 collective-permute-start.27
  83.6 2.3 convolution_convert_fusion.7
  91.1 3.8 collective-permute-done.26
  94.9 6.1 %collective-permute-done.28 = bf16[128,1024]{1,0:T(8,128)(2,1)S(1)} collective-permute-done((bf16[128,1024]{1,0:T(8,128)(2,1)S(1)}, bf16[128,1024]{1,0:T(8,128)(2,1)S(1)}, u32[]{:S(2)}, u32[]{:S(2)}) %collective-permute-start.28) | collective-permute-done | bytes 262176 | tf_op jit(solution)/shard_map/ppermute | solution.py:285
  101.0 4.1 %collective-permute-done.23 = bf16[192,1024]{1,0:T(8,128)(2,1)S(1)} collective-permute-done((bf16[192,1024]{1,0:T(8,128)(2,1)S(1)}, bf16[192,1024]{1,0:T(8,128)(2,1)S(1)}, u32[]{:S(2)}, u32[]{:S(2)}) %collective-permute-start.23) | collective-permute-done | bytes 393248 | tf_op jit(solution)/shard_map/ppermute | solution.py:291
  109.2 6.8 %collective-permute-done.24 = bf16[192,1024]{1,0:T(8,128)(2,1)S(1)} collective-permute-done((bf16[192,1024]{1,0:T(8,128)(2,1)S(1)}, bf16[192,1024]{1,0:T(8,128)(2,1)S(1)}, u32[]{:S(2)}, u32[]{:S(2)}) %collective-permute-start.24) | collective-permute-done | bytes 393248 | tf_op jit(solution)/shard_map/ppermute | solution.py:291
  118.4 21.7 %collective-permute-done.32 = bf16[128,1024]{1,0:T(8,128)(2,1)S(1)} collective-permute-done((bf16[128,1024]{1,0:T(8,128)(2,1)}, bf16[128,1024]{1,0:T(8,128)(2,1)S(1)}, u32[]{:S(2)}, u32[]{:S(2)}) %collective-permute-start.32) | collective-permute-done | bytes 262176 | tf_op jit(solution)/shard_map/ppermute | solution.py:285
  141.2 2.2 collective-permute-start.33
  143.4 1.9 collective-permute-start.34
  145.6 1.6 multiply_convert_fusion
  147.3 6.4 %multiply_convert_fusion.1 = (bf16[768,1024]{1,0:T(8,128)(2,1)S(1)}, f32[768,1024]{1,0:T(8,128)}) fusion(f32[1024]{0:T(1024)S(1)} %dynamic_slice.48, bf16[512,1024]{1,0:T(8,128)(2,1)} %collective-permute-done.29, bf16[512,1024]{1,0:T(8,128)(2,1)} %pad_maximum_fusion.4, bf16[384,1024]{1,0:T(8,128)(2,1)} %collective-permute-done.25, ...), kind=kOutput, calls=%fused_computation.41 | convolution fusion | flops 1627389952 | bytes 8392704 | tf_op jit(solution)/shard_map/dot_general | solution.py:42
  153.7 15.2 %collective-permute-done.33.refs_1_ = bf16[256,1024]{1,0:T(8,128)(2,1)S(1)} collective-permute-done((bf16[256,1024]{1,0:T(8,128)(2,1)S(1)}, bf16[256,1024]{1,0:T(8,128)(2,1)S(1)}, u32[]{:S(2)}, u32[]{:S(2)}) %collective-permute-start.33) | collective-permute-done | bytes 524320 | tf_op jit(solution)/shard_map/ppermute | solution.py:285
  168.9 10.2 %collective-permute-done.35.refs_3_ = bf16[256,1024]{1,0:T(8,128)(2,1)S(1)} collective-permute-done((bf16[256,1024]{1,0:T(8,128)(2,1)S(1)}, bf16[256,1024]{1,0:T(8,128)(2,1)S(1)}, u32[]{:S(2)}, u32[]{:S(2)}) %collective-permute-start.35) | collective-permute-done | bytes 524320 | tf_op jit(solution)/shard_map/ppermute | solution.py:285
  179.9 2.0 convolution_convert_fusion.1
  181.9 3.0 assemble.1
  184.9 6.6 %fusion.159 = (f32[1024]{0:T(1024)S(1)}, bf16[768,1024]{1,0:T(8,128)(2,1)S(1)}) fusion(f32[768,1024]{1,0:T(8,128)} %get-tuple-element.192, f32[1024]{0:T(1024)S(1)} %dynamic_slice.48, bf16[768,1024]{1,0:T(8,128)(2,1)} %copy-done.21, bf16[1024,1024]{1,0:T(8,128)(2,1)} %assemble.1), kind=kOutput, calls=%fused_computation.342 | convolution fusion | flops 1627913216 | bytes 8396800 | tf_op jit(solution)/shard_map/dot_general | solution.py:42
  191.5 4.0 %convolution_convert_fusion.5 = bf16[384,1024]{1,0:T(8,128)(2,1)} fusion(bf16[768,1024]{1,0:T(8,128)(2,1)S(1)} %get-tuple-element.80, bf16[512,1024]{1,0:T(8,128)(2,1)} %collective-permute-done.29, bf16[512,1024]{1,0:T(8,128)(2,1)} %pad_maximum_fusion.4), kind=kOutput, calls=%fused_computation.58 | convolution fusion | flops 809893888 | bytes 3670016 | tf_op jit(solution)/shard_map/dot_general | solution.py:42
  198.0 2.9 convert_add_fusion.2
  205.4 2.4 fusion.32
  207.8 7.2 %collective-permute-done.39 = bf16[192,1024]{1,0:T(8,128)(2,1)S(1)} collective-permute-done((bf16[192,1024]{1,0:T(8,128)(2,1)S(1)}, bf16[192,1024]{1,0:T(8,128)(2,1)S(1)}, u32[]{:S(2)}, u32[]{:S(2)}) %collective-permute-start.39) | collective-permute-done | bytes 393248 | tf_op jit(solution)/shard_map/ppermute | solution.py:291
  218.4 8.5 %collective-permute-done.40 = bf16[192,1024]{1,0:T(8,128)(2,1)S(1)} collective-permute-done((bf16[192,1024]{1,0:T(8,128)(2,1)S(1)}, bf16[192,1024]{1,0:T(8,128)(2,1)S(1)}, u32[]{:S(2)}, u32[]{:S(2)}) %collective-permute-start.40) | collective-permute-done | bytes 393248 | tf_op jit(solution)/shard_map/ppermute | solution.py:291
  227.0 2.0 convolution_convert_fusion
  231.4 12.4 %collective-permute-start.67 = (bf16[128,1024]{1,0:T(8,128)(2,1)}, bf16[128,1024]{1,0:T(8,128)(2,1)}, u32[]{:S(2)}, u32[]{:S(2)}) collective-permute-start(bf16[128,1024]{1,0:T(8,128)(2,1)} %get-tuple-element.147), channel_id=1, source_target_pairs={{0,16},{4,20},{8,24},{12,28},{16,0},{20,4},{24,8},{28,12},{1,17},{... | collective-permute-start | bytes 786440 | tf_op jit(solution)/shard_map/ppermute | solution.py:285
  249.9 10.7 %attend_back.1 = (bf16[768,768]{1,0:T(8,128)(2,1)}, f32[16,128]{1,0:T(8,128)}) custom-call(bf16[768,768]{1,0:T(8,128)(2,1)} %get-tuple-element.52.refs_0_.refs_1_.refs_2_, bf16[768,768]{1,0:T(8,128)(2,1)} %get-tuple-element.52.refs_0_.refs_1_.refs_2_, bf16[768,768]{1,0:T(8,128)(2,1)} %get-tuple-element.52.refs_0_.refs_1_.refs_2_, ...), custom_call_target="tpu_custom_call" | custom-call | flops 1000 | bytes 1000 | tf_op jit(solution)/shard_map/attend_back/pallas_call | solution.py:229
  260.6 2.5 convolution_convert_fusion.2
  268.9 3.0 collective-permute-start.65
  272.0 2.2 fusion.27
  275.4 7.0 %collective-permute-done.63 = bf16[128,1024]{1,0:T(8,128)(2,1)S(1)} collective-permute-done((bf16[128,1024]{1,0:T(8,128)(2,1)S(1)}, bf16[128,1024]{1,0:T(8,128)(2,1)S(1)}, u32[]{:S(2)}, u32[]{:S(2)}) %collective-permute-start.63) | collective-permute-done | bytes 262176 | tf_op jit(solution)/shard_map/ppermute | solution.py:285
  282.4 6.1 %collective-permute-done.64 = bf16[128,1024]{1,0:T(8,128)(2,1)S(1)} collective-permute-done((bf16[128,1024]{1,0:T(8,128)(2,1)S(1)}, bf16[128,1024]{1,0:T(8,128)(2,1)S(1)}, u32[]{:S(2)}, u32[]{:S(2)}) %collective-permute-start.64) | collective-permute-done | bytes 262176 | tf_op jit(solution)/shard_map/ppermute | solution.py:285
  289.7 2.0 convert_add_fusion
  291.8 2.3 fusion.15
  294.1 1.7 fusion.112
  298.7 3.6 fusion.43
  306.2 3.8 %collective-permute-start.50 = (f32[1,7168]{1,0:T(1,128)S(1)}, f32[1,7168]{1,0:T(1,128)S(1)}, u32[]{:S(2)}, u32[]{:S(2)}) collective-permute-start(f32[1,7168]{1,0:T(1,128)S(1)} %bitcast.157), channel_id=1, source_target_pairs={{0,24},{4,28},{8,16},{12,20},{16,8},{20,12},{24,0},{28,4},{1,25},{... | collective-permute-start | bytes 86024 | tf_op jit(solution)/shard_map/ppermute | solution.py:285
  310.0 2.9 collective-permute-start.49
  313.7 2.0 constant_dynamic-update-slice_fusion.13
  315.7 2.1 fusion.80
  321.3 4.4 %collective-permute-done.51 = f32[4,7168]{1,0:T(4,128)S(1)} collective-permute-done((f32[4,7168]{1,0:T(4,128)S(1)}, f32[4,7168]{1,0:T(4,128)S(1)}, u32[]{:S(2)}, u32[]{:S(2)}) %collective-permute-start.51) | collective-permute-done | bytes 114720 | tf_op jit(solution)/shard_map/ppermute | solution.py:285
  331.2 2.2 collective-permute-done.53
  334.9 3.0 collective-permute-done.54
  337.9 2.1 collective-permute-start.55
  340.0 1.6 collective-permute-done.55
  343.0 4.0 %collective-permute-done.56 = f32[1,2,128]{2,0,1:T(1,128)S(1)} collective-permute-done((f32[1,2,128]{2,0,1:T(1,128)S(1)}, f32[1,2,128]{2,0,1:T(1,128)S(1)}, u32[]{:S(2)}, u32[]{:S(2)}) %collective-permute-start.56) | collective-permute-done | bytes 1056 | tf_op jit(solution)/shard_map/ppermute | solution.py:285
  347.6 1.6 fusion.74
  350.7 3.0 collective-permute-start.58
  354.8 1.6 fusion.97
  361.9 7.9 %collective-permute-done.58 = bf16[128,1024]{1,0:T(8,128)(2,1)S(1)} collective-permute-done((bf16[128,1024]{1,0:T(8,128)(2,1)S(1)}, bf16[128,1024]{1,0:T(8,128)(2,1)S(1)}, u32[]{:S(2)}, u32[]{:S(2)}) %collective-permute-start.58) | collective-permute-done | bytes 262176 | tf_op jit(solution)/shard_map/ppermute | solution.py:285
  371.9 4.2 %collective-permute-done.61 = bf16[64,1024]{1,0:T(8,128)(2,1)S(1)} collective-permute-done((bf16[64,1024]{1,0:T(8,128)(2,1)S(1)}, bf16[64,1024]{1,0:T(8,128)(2,1)S(1)}, u32[]{:S(2)}, u32[]{:S(2)}) %collective-permute-start.61) | collective-permute-done | bytes 131104 | tf_op jit(solution)/shard_map/ppermute | solution.py:291
  (469 shorter events, 101.9 us)
Async XLA Ops:
  0.7 11.9 %collective-permute-start.2 = (bf16[1,1024]{1,0:T(2,128)(2,1)}, bf16[1,1024]{1,0:T(2,128)(2,1)S(1)}, u32[]{:S(2)}, u32[]{:S(2)}) collective-permute-start(bf16[1,1024]{1,0:T(2,128)(2,1)} %param.14), channel_id=1, source_target_pairs={{0,24},{4,28},{8,16},{12,20},{16,8},{20,12},{24,0},{28,4},{1,25},{... | collective-permute-start | bytes 6152 | tf_op jit(solution)/shard_map/ppermute | solution.py:285
  5.8 6.7 %collective-permute-start.1 = (bf16[1,1024]{1,0:T(2,128)(2,1)}, bf16[1,1024]{1,0:T(2,128)(2,1)S(1)}, u32[]{:S(2)}, u32[]{:S(2)}) collective-permute-start(bf16[1,1024]{1,0:T(2,128)(2,1)} %param.14), channel_id=1, source_target_pairs={{0,8},{4,12},{8,0},{12,4},{16,24},{20,28},{24,16},{28,20},{1,9},{5... | collective-permute-start | bytes 6152 | tf_op jit(solution)/shard_map/ppermute | solution.py:285
  5.8 6.7 %collective-permute-start = (bf16[1,1024]{1,0:T(2,128)(2,1)}, bf16[1,1024]{1,0:T(2,128)(2,1)S(1)}, u32[]{:S(2)}, u32[]{:S(2)}) collective-permute-start(bf16[1,1024]{1,0:T(2,128)(2,1)} %param.14), channel_id=1, source_target_pairs={{0,16},{4,20},{8,24},{12,28},{16,0},{20,4},{24,8},{28,12},{1,17},{... | collective-permute-start | bytes 6152 | tf_op jit(solution)/shard_map/ppermute | solution.py:285
  8.3 21.5 %collective-permute-start.9 = (bf16[192,1024]{1,0:T(8,128)(2,1)S(1)}, bf16[192,1024]{1,0:T(8,128)(2,1)S(1)}, u32[]{:S(2)}, u32[]{:S(2)}) collective-permute-start(bf16[192,1024]{1,0:T(8,128)(2,1)S(1)} %convolution_convert_fusion.8), channel_id=1, source_target_pairs={{0,2},{2,0},{1,3},{3,1},{4,6},{6,4},{5,7},{7,5},{8,10},{10,8},{9,1... | collective-permute-start | bytes 1179656 | tf_op jit(solution)/shard_map/ppermute | solution.py:291
  10.3 29.4 %collective-permute-start.11 = (bf16[128,768]{1,0:T(8,128)(2,1)S(1)}, bf16[128,768]{1,0:T(8,128)(2,1)}, u32[]{:S(2)}, u32[]{:S(2)}) collective-permute-start(bf16[128,768]{1,0:T(8,128)(2,1)S(1)} %copy.48.refs_4_), channel_id=1, source_target_pairs={{0,16},{4,20},{8,24},{12,28},{16,0},{20,4},{24,8},{28,12},{1,17},{... | collective-permute-start | bytes 589832 | tf_op jit(solution)/shard_map/ppermute | solution.py:285
  16.7 4.2 %collective-permute-start.4 = (f32[4,3072]{1,0:T(4,128)S(1)}, f32[4,3072]{1,0:T(4,128)S(1)}, u32[]{:S(2)}, u32[]{:S(2)}) collective-permute-start(f32[4,3072]{1,0:T(4,128)S(1)} %slice.528), channel_id=1, source_target_pairs={{0,4},{4,0},{8,12},{12,8},{16,20},{20,16},{24,28},{28,24},{1,5},{5... | collective-permute-start | bytes 147464 | tf_op jit(solution)/shard_map/ppermute | solution.py:285
  20.9 5.7 %collective-permute-start.7 = (f32[1,3072]{1,0:T(1,128)S(1)}, f32[1,3072]{1,0:T(1,128)S(1)}, u32[]{:S(2)}, u32[]{:S(2)}) collective-permute-start(f32[1,3072]{1,0:T(1,128)S(1)} %get-tuple-element.167), channel_id=1, source_target_pairs={{0,24},{4,28},{8,16},{12,20},{16,8},{20,12},{24,0},{28,4},{1,25},{... | collective-permute-start | bytes 36872 | tf_op jit(solution)/shard_map/ppermute | solution.py:285
  22.4 4.6 %collective-permute-start.6 = (f32[1,3072]{1,0:T(1,128)S(1)}, f32[1,3072]{1,0:T(1,128)S(1)}, u32[]{:S(2)}, u32[]{:S(2)}) collective-permute-start(f32[1,3072]{1,0:T(1,128)S(1)} %get-tuple-element.168), channel_id=1, source_target_pairs={{0,8},{4,12},{8,0},{12,4},{16,24},{20,28},{24,16},{28,20},{1,9},{5... | collective-permute-start | bytes 36872 | tf_op jit(solution)/shard_map/ppermute | solution.py:285
  23.0 5.5 %collective-permute-start.5 = (f32[1,3072]{1,0:T(1,128)S(1)}, f32[1,3072]{1,0:T(1,128)S(1)}, u32[]{:S(2)}, u32[]{:S(2)}) collective-permute-start(f32[1,3072]{1,0:T(1,128)S(1)} %get-tuple-element.166), channel_id=1, source_target_pairs={{0,16},{4,20},{8,24},{12,28},{16,0},{20,4},{24,8},{28,12},{1,17},{... | collective-permute-start | bytes 36872 | tf_op jit(solution)/shard_map/ppermute | solution.py:285
  26.6 13.7 %collective-permute-start.12 = (bf16[128,768]{1,0:T(8,128)(2,1)S(1)}, bf16[128,768]{1,0:T(8,128)(2,1)S(1)}, u32[]{:S(2)}, u32[]{:S(2)}) collective-permute-start(bf16[128,768]{1,0:T(8,128)(2,1)S(1)} %copy.48.refs_4_), channel_id=1, source_target_pairs={{0,8},{4,12},{8,0},{12,4},{16,24},{20,28},{24,16},{28,20},{1,9},{5... | collective-permute-start | bytes 589832 | tf_op jit(solution)/shard_map/ppermute | solution.py:285
  27.0 14.8 %collective-permute-start.13 = (bf16[128,768]{1,0:T(8,128)(2,1)S(1)}, bf16[128,768]{1,0:T(8,128)(2,1)S(1)}, u32[]{:S(2)}, u32[]{:S(2)}) collective-permute-start(bf16[128,768]{1,0:T(8,128)(2,1)S(1)} %copy.48.refs_4_), channel_id=1, source_target_pairs={{0,24},{4,28},{8,16},{12,20},{16,8},{20,12},{24,0},{28,4},{1,25},{... | collective-permute-start | bytes 589832 | tf_op jit(solution)/shard_map/ppermute | solution.py:285
  30.7 19.0 %collective-permute-start.10 = (bf16[384,1024]{1,0:T(8,128)(2,1)}, bf16[384,1024]{1,0:T(8,128)(2,1)}, u32[]{:S(2)}, u32[]{:S(2)}) collective-permute-start(bf16[384,1024]{1,0:T(8,128)(2,1)} %pad_maximum_fusion.6), channel_id=1, source_target_pairs={{0,1},{1,0},{2,3},{3,2},{4,5},{5,4},{6,7},{7,6},{8,9},{9,8},{10,11... | collective-permute-start | bytes 2359304 | tf_op jit(solution)/shard_map/ppermute | solution.py:294
  37.1 7.8 %collective-permute-start.14 = (bf16[128,768]{1,0:T(8,128)(2,1)S(1)}, bf16[128,768]{1,0:T(8,128)(2,1)S(1)}, u32[]{:S(2)}, u32[]{:S(2)}) collective-permute-start(bf16[128,768]{1,0:T(8,128)(2,1)S(1)} %copy.48.refs_4_), channel_id=1, source_target_pairs={{0,4},{4,0},{8,12},{12,8},{16,20},{20,16},{24,28},{28,24},{1,5},{5... | collective-permute-start | bytes 589832 | tf_op jit(solution)/shard_map/ppermute | solution.py:285
  39.7 9.3 %collective-permute-start.15 = (bf16[128,768]{1,0:T(8,128)(2,1)}, bf16[128,768]{1,0:T(8,128)(2,1)S(1)}, u32[]{:S(2)}, u32[]{:S(2)}) collective-permute-start(bf16[128,768]{1,0:T(8,128)(2,1)} %collective-permute-done.11.refs_5_), channel_id=1, source_target_pairs={{0,4},{4,0},{8,12},{12,8},{16,20},{20,16},{24,28},{28,24},{1,5},{5... | collective-permute-start | bytes 589832 | tf_op jit(solution)/shard_map/ppermute | solution.py:285
  40.3 15.4 %collective-permute-start.16 = (bf16[128,768]{1,0:T(8,128)(2,1)S(1)}, bf16[128,768]{1,0:T(8,128)(2,1)S(1)}, u32[]{:S(2)}, u32[]{:S(2)}) collective-permute-start(bf16[128,768]{1,0:T(8,128)(2,1)S(1)} %collective-permute-done.12.refs_6_), channel_id=1, source_target_pairs={{0,4},{4,0},{8,12},{12,8},{16,20},{20,16},{24,28},{28,24},{1,5},{5... | collective-permute-start | bytes 589832 | tf_op jit(solution)/shard_map/ppermute | solution.py:285
  41.8 15.0 %collective-permute-start.17 = (bf16[128,768]{1,0:T(8,128)(2,1)S(1)}, bf16[128,768]{1,0:T(8,128)(2,1)S(1)}, u32[]{:S(2)}, u32[]{:S(2)}) collective-permute-start(bf16[128,768]{1,0:T(8,128)(2,1)S(1)} %collective-permute-done.13.refs_7_), channel_id=1, source_target_pairs={{0,4},{4,0},{8,12},{12,8},{16,20},{20,16},{24,28},{28,24},{1,5},{5... | collective-permute-start | bytes 589832 | tf_op jit(solution)/shard_map/ppermute | solution.py:285
  44.8 19.1 %collective-permute-start.18 = (bf16[128,256]{0,1:T(8,128)(2,1)S(1)}, bf16[128,256]{0,1:T(8,128)(2,1)S(1)}, u32[]{:S(2)}, u32[]{:S(2)}) collective-permute-start(bf16[128,256]{0,1:T(8,128)(2,1)S(1)} %dynamic-slice_bitcast_fusion.3), channel_id=1, source_target_pairs={{0,16},{4,20},{8,24},{12,28},{16,0},{20,4},{24,8},{28,12},{1,17},{... | collective-permute-start | bytes 196616 | tf_op jit(solution)/shard_map/ppermute | solution.py:285
  49.0 14.8 %collective-permute-start.19 = (bf16[128,256]{0,1:T(8,128)(2,1)S(1)}, bf16[128,256]{0,1:T(8,128)(2,1)S(1)}, u32[]{:S(2)}, u32[]{:S(2)}) collective-permute-start(bf16[128,256]{0,1:T(8,128)(2,1)S(1)} %dynamic-slice_bitcast_fusion.3), channel_id=1, source_target_pairs={{0,8},{4,12},{8,0},{12,4},{16,24},{20,28},{24,16},{28,20},{1,9},{5... | collective-permute-start | bytes 196616 | tf_op jit(solution)/shard_map/ppermute | solution.py:285
  49.8 14.1 %collective-permute-start.20 = (bf16[128,256]{0,1:T(8,128)(2,1)S(1)}, bf16[128,256]{0,1:T(8,128)(2,1)S(1)}, u32[]{:S(2)}, u32[]{:S(2)}) collective-permute-start(bf16[128,256]{0,1:T(8,128)(2,1)S(1)} %dynamic-slice_bitcast_fusion.3), channel_id=1, source_target_pairs={{0,24},{4,28},{8,16},{12,20},{16,8},{20,12},{24,0},{28,4},{1,25},{... | collective-permute-start | bytes 196616 | tf_op jit(solution)/shard_map/ppermute | solution.py:285
  64.0 12.8 %collective-permute-start.21 = (bf16[512,256]{0,1:T(8,128)(2,1)S(1)}, bf16[512,256]{0,1:T(8,128)(2,1)S(1)}, u32[]{:S(2)}, u32[]{:S(2)}) collective-permute-start(bf16[512,256]{0,1:T(8,128)(2,1)S(1)} %pad_maximum_fusion.18), channel_id=1, source_target_pairs={{0,4},{4,0},{8,12},{12,8},{16,20},{20,16},{24,28},{28,24},{1,5},{5... | collective-permute-start | bytes 786440 | tf_op jit(solution)/shard_map/ppermute | solution.py:285
  79.0 7.5 %collective-permute-start.22 = (bf16[384,1024]{1,0:T(8,128)(2,1)}, bf16[384,1024]{1,0:T(8,128)(2,1)}, u32[]{:S(2)}, u32[]{:S(2)}) collective-permute-start(bf16[384,1024]{1,0:T(8,128)(2,1)} %convolution_convert_fusion.3), channel_id=1, source_target_pairs={{0,1},{1,0},{2,3},{3,2},{4,5},{5,4},{6,7},{7,6},{8,9},{9,8},{10,11... | collective-permute-start | bytes 2359304 | tf_op jit(solution)/shard_map/ppermute | solution.py:294
  79.1 15.8 %collective-permute-start.26 = (bf16[128,1024]{1,0:T(8,128)(2,1)S(1)}, bf16[128,1024]{1,0:T(8,128)(2,1)S(1)}, u32[]{:S(2)}, u32[]{:S(2)}) collective-permute-start(bf16[128,1024]{1,0:T(8,128)(2,1)S(1)} %constant_dynamic-slice_fusion.3), channel_id=1, source_target_pairs={{0,16},{4,20},{8,24},{12,28},{16,0},{20,4},{24,8},{28,12},{1,17},{... | collective-permute-start | bytes 786440 | tf_op jit(solution)/shard_map/ppermute | solution.py:285
  80.7 14.2 %collective-permute-start.27 = (bf16[128,1024]{1,0:T(8,128)(2,1)S(1)}, bf16[128,1024]{1,0:T(8,128)(2,1)S(1)}, u32[]{:S(2)}, u32[]{:S(2)}) collective-permute-start(bf16[128,1024]{1,0:T(8,128)(2,1)S(1)} %constant_dynamic-slice_fusion.3), channel_id=1, source_target_pairs={{0,8},{4,12},{8,0},{12,4},{16,24},{20,28},{24,16},{28,20},{1,9},{5... | collective-permute-start | bytes 786440 | tf_op jit(solution)/shard_map/ppermute | solution.py:285
  83.2 17.8 %collective-permute-start.28 = (bf16[128,1024]{1,0:T(8,128)(2,1)S(1)}, bf16[128,1024]{1,0:T(8,128)(2,1)S(1)}, u32[]{:S(2)}, u32[]{:S(2)}) collective-permute-start(bf16[128,1024]{1,0:T(8,128)(2,1)S(1)} %constant_dynamic-slice_fusion.3), channel_id=1, source_target_pairs={{0,24},{4,28},{8,16},{12,20},{16,8},{20,12},{24,0},{28,4},{1,25},{... | collective-permute-start | bytes 786440 | tf_op jit(solution)/shard_map/ppermute | solution.py:285
  85.9 15.1 %collective-permute-start.30 = (bf16[192,1024]{1,0:T(8,128)(2,1)S(1)}, bf16[192,1024]{1,0:T(8,128)(2,1)S(1)}, u32[]{:S(2)}, u32[]{:S(2)}) collective-permute-start(bf16[192,1024]{1,0:T(8,128)(2,1)S(1)} %convolution_convert_fusion.7), channel_id=1, source_target_pairs={{0,2},{2,0},{1,3},{3,1},{4,6},{6,4},{5,7},{7,5},{8,10},{10,8},{9,1... | collective-permute-start | bytes 1179656 | tf_op jit(solution)/shard_map/ppermute | solution.py:291
  88.1 17.0 %collective-permute-start.23 = (bf16[192,1024]{1,0:T(8,128)(2,1)S(1)}, bf16[192,1024]{1,0:T(8,128)(2,1)S(1)}, u32[]{:S(2)}, u32[]{:S(2)}) collective-permute-start(bf16[192,1024]{1,0:T(8,128)(2,1)S(1)} %slice.853), channel_id=1, source_target_pairs={{0,2},{2,0},{1,3},{3,1},{4,6},{6,4},{5,7},{7,5},{8,10},{10,8},{9,1... | collective-permute-start | bytes 1179656 | tf_op jit(solution)/shard_map/ppermute | solution.py:291
  106.1 9.9 %collective-permute-start.24 = (bf16[192,1024]{1,0:T(8,128)(2,1)S(1)}, bf16[192,1024]{1,0:T(8,128)(2,1)S(1)}, u32[]{:S(2)}, u32[]{:S(2)}) collective-permute-start(bf16[192,1024]{1,0:T(8,128)(2,1)S(1)} %add_convert_fusion), channel_id=1, source_target_pairs={{0,2},{2,0},{1,3},{3,1},{4,6},{6,4},{5,7},{7,5},{8,10},{10,8},{9,1... | collective-permute-start | bytes 1179656 | tf_op jit(solution)/shard_map/ppermute | solution.py:291
  107.6 37.7 %collective-permute-start.31 = (bf16[384,1024]{1,0:T(8,128)(2,1)}, bf16[384,1024]{1,0:T(8,128)(2,1)}, u32[]{:S(2)}, u32[]{:S(2)}) collective-permute-start(bf16[384,1024]{1,0:T(8,128)(2,1)} %pad_maximum_fusion.8), channel_id=1, source_target_pairs={{0,1},{1,0},{2,3},{3,2},{4,5},{5,4},{6,7},{7,6},{8,9},{9,8},{10,11... | collective-permute-start | bytes 2359304 | tf_op jit(solution)/shard_map/ppermute | solution.py:294
  108.7 38.6 %collective-permute-start.29 = (bf16[512,1024]{1,0:T(8,128)(2,1)}, bf16[512,1024]{1,0:T(8,128)(2,1)}, u32[]{:S(2)}, u32[]{:S(2)}) collective-permute-start(bf16[512,1024]{1,0:T(8,128)(2,1)} %pad_maximum_fusion.4), channel_id=1, source_target_pairs={{0,4},{4,0},{8,12},{12,8},{16,20},{20,16},{24,28},{28,24},{1,5},{5... | collective-permute-start | bytes 3145736 | tf_op jit(solution)/shard_map/ppermute | solution.py:285
  117.0 30.3 %collective-permute-start.25 = (bf16[384,1024]{1,0:T(8,128)(2,1)}, bf16[384,1024]{1,0:T(8,128)(2,1)}, u32[]{:S(2)}, u32[]{:S(2)}) collective-permute-start(bf16[384,1024]{1,0:T(8,128)(2,1)} %pad_maximum_fusion.7), channel_id=1, source_target_pairs={{0,1},{1,0},{2,3},{3,2},{4,5},{5,4},{6,7},{7,6},{8,9},{9,8},{10,11... | collective-permute-start | bytes 2359304 | tf_op jit(solution)/shard_map/ppermute | solution.py:294
  117.8 22.3 %collective-permute-start.32 = (bf16[128,1024]{1,0:T(8,128)(2,1)}, bf16[128,1024]{1,0:T(8,128)(2,1)S(1)}, u32[]{:S(2)}, u32[]{:S(2)}) collective-permute-start(bf16[128,1024]{1,0:T(8,128)(2,1)} %bitcast.150), channel_id=1, source_target_pairs={{0,4},{4,0},{8,12},{12,8},{16,20},{20,16},{24,28},{28,24},{1,5},{5... | collective-permute-start | bytes 786440 | tf_op jit(solution)/shard_map/ppermute | solution.py:285
  141.2 27.7 %collective-permute-start.33 = (bf16[256,1024]{1,0:T(8,128)(2,1)S(1)}, bf16[256,1024]{1,0:T(8,128)(2,1)S(1)}, u32[]{:S(2)}, u32[]{:S(2)}) collective-permute-start(bf16[256,1024]{1,0:T(8,128)(2,1)S(1)} %pad_maximum_fusion.15.refs_0_), channel_id=1, source_target_pairs={{0,16},{4,20},{8,24},{12,28},{16,0},{20,4},{24,8},{28,12},{1,17},{... | collective-permute-start | bytes 1572872 | tf_op jit(solution)/shard_map/ppermute | solution.py:285
  143.4 25.5 %collective-permute-start.34 = (bf16[256,1024]{1,0:T(8,128)(2,1)S(1)}, bf16[256,1024]{1,0:T(8,128)(2,1)S(1)}, u32[]{:S(2)}, u32[]{:S(2)}) collective-permute-start(bf16[256,1024]{1,0:T(8,128)(2,1)S(1)} %pad_maximum_fusion.15.refs_0_), channel_id=1, source_target_pairs={{0,8},{4,12},{8,0},{12,4},{16,24},{20,28},{24,16},{28,20},{1,9},{5... | collective-permute-start | bytes 1572872 | tf_op jit(solution)/shard_map/ppermute | solution.py:285
  145.3 33.8 %collective-permute-start.35 = (bf16[256,1024]{1,0:T(8,128)(2,1)S(1)}, bf16[256,1024]{1,0:T(8,128)(2,1)S(1)}, u32[]{:S(2)}, u32[]{:S(2)}) collective-permute-start(bf16[256,1024]{1,0:T(8,128)(2,1)S(1)} %pad_maximum_fusion.15.refs_0_), channel_id=1, source_target_pairs={{0,24},{4,28},{8,16},{12,20},{16,8},{20,12},{24,0},{28,4},{1,25},{... | collective-permute-start | bytes 1572872 | tf_op jit(solution)/shard_map/ppermute | solution.py:285
  196.1 34.2 %collective-permute-start.66 = (bf16[512,1024]{1,0:T(8,128)(2,1)}, bf16[512,1024]{1,0:T(8,128)(2,1)S(1)}, u32[]{:S(2)}, u32[]{:S(2)}) collective-permute-start(bf16[512,1024]{1,0:T(8,128)(2,1)} %convolution_convert_fusion.1), channel_id=1, source_target_pairs={{0,4},{4,0},{8,12},{12,8},{16,20},{20,16},{24,28},{28,24},{1,5},{5... | collective-permute-start | bytes 3145736 | tf_op jit(solution)/shard_map/ppermute | solution.py:285
  203.4 40.4 %collective-permute-start.37 = (bf16[384,1024]{1,0:T(8,128)(2,1)S(1)}, bf16[384,1024]{1,0:T(8,128)(2,1)S(1)}, u32[]{:S(2)}, u32[]{:S(2)}) collective-permute-start(bf16[384,1024]{1,0:T(8,128)(2,1)S(1)} %convolution_convert_fusion.4), channel_id=1, source_target_pairs={{0,1},{1,0},{2,3},{3,2},{4,5},{5,4},{6,7},{7,6},{8,9},{9,8},{10,11... | collective-permute-start | bytes 2359304 | tf_op jit(solution)/shard_map/ppermute | solution.py:294
  203.6 11.4 %collective-permute-start.39 = (bf16[192,1024]{1,0:T(8,128)(2,1)S(1)}, bf16[192,1024]{1,0:T(8,128)(2,1)S(1)}, u32[]{:S(2)}, u32[]{:S(2)}) collective-permute-start(bf16[192,1024]{1,0:T(8,128)(2,1)S(1)} %slice.851), channel_id=1, source_target_pairs={{0,2},{2,0},{1,3},{3,1},{4,6},{6,4},{5,7},{7,5},{8,10},{10,8},{9,1... | collective-permute-start | bytes 1179656 | tf_op jit(solution)/shard_map/ppermute | solution.py:291
  216.3 10.6 %collective-permute-start.40 = (bf16[192,1024]{1,0:T(8,128)(2,1)S(1)}, bf16[192,1024]{1,0:T(8,128)(2,1)S(1)}, u32[]{:S(2)}, u32[]{:S(2)}) collective-permute-start(bf16[192,1024]{1,0:T(8,128)(2,1)S(1)} %multiply_convert_fusion.2), channel_id=1, source_target_pairs={{0,2},{2,0},{1,3},{3,1},{4,6},{6,4},{5,7},{7,5},{8,10},{10,8},{9,1... | collective-permute-start | bytes 1179656 | tf_op jit(solution)/shard_map/ppermute | solution.py:291
  226.9 20.3 %collective-permute-start.41 = (bf16[384,1024]{1,0:T(8,128)(2,1)S(1)}, bf16[384,1024]{1,0:T(8,128)(2,1)S(1)}, u32[]{:S(2)}, u32[]{:S(2)}) collective-permute-start(bf16[384,1024]{1,0:T(8,128)(2,1)S(1)} %pad_maximum_fusion.9), channel_id=1, source_target_pairs={{0,1},{1,0},{2,3},{3,2},{4,5},{5,4},{6,7},{7,6},{8,9},{9,8},{10,11... | collective-permute-start | bytes 2359304 | tf_op jit(solution)/shard_map/ppermute | solution.py:294
  229.0 37.0 %collective-permute-start.62 = (bf16[512,1024]{1,0:T(8,128)(2,1)}, bf16[512,1024]{1,0:T(8,128)(2,1)}, u32[]{:S(2)}, u32[]{:S(2)}) collective-permute-start(bf16[512,1024]{1,0:T(8,128)(2,1)} %convolution_convert_fusion), channel_id=1, source_target_pairs={{0,4},{4,0},{8,12},{12,8},{16,20},{20,16},{24,28},{28,24},{1,5},{5... | collective-permute-start | bytes 3145736 | tf_op jit(solution)/shard_map/ppermute | solution.py:285
  231.4 74.7 %collective-permute-start.67 = (bf16[128,1024]{1,0:T(8,128)(2,1)}, bf16[128,1024]{1,0:T(8,128)(2,1)}, u32[]{:S(2)}, u32[]{:S(2)}) collective-permute-start(bf16[128,1024]{1,0:T(8,128)(2,1)} %get-tuple-element.147), channel_id=1, source_target_pairs={{0,16},{4,20},{8,24},{12,28},{16,0},{20,4},{24,8},{28,12},{1,17},{... | collective-permute-start | bytes 786440 | tf_op jit(solution)/shard_map/ppermute | solution.py:285
  245.7 19.5 %collective-permute-start.38 = (bf16[192,1024]{1,0:T(8,128)(2,1)}, bf16[192,1024]{1,0:T(8,128)(2,1)}, u32[]{:S(2)}, u32[]{:S(2)}) collective-permute-start(bf16[192,1024]{1,0:T(8,128)(2,1)} %slice.852), channel_id=1, source_target_pairs={{0,2},{2,0},{1,3},{3,1},{4,6},{6,4},{5,7},{7,5},{8,10},{10,8},{9,1... | collective-permute-start | bytes 1179656 | tf_op jit(solution)/shard_map/ppermute | solution.py:291
  265.1 24.7 %collective-permute-start.45 = (bf16[384,1024]{1,0:T(8,128)(2,1)S(1)}, bf16[384,1024]{1,0:T(8,128)(2,1)S(1)}, u32[]{:S(2)}, u32[]{:S(2)}) collective-permute-start(bf16[384,1024]{1,0:T(8,128)(2,1)S(1)} %get-tuple-element.160), channel_id=1, source_target_pairs={{0,1},{1,0},{2,3},{3,2},{4,5},{5,4},{6,7},{7,6},{8,9},{9,8},{10,11... | collective-permute-start | bytes 2359304 | tf_op jit(solution)/shard_map/ppermute | solution.py:294
  267.5 14.9 %collective-permute-start.63 = (bf16[128,1024]{1,0:T(8,128)(2,1)S(1)}, bf16[128,1024]{1,0:T(8,128)(2,1)S(1)}, u32[]{:S(2)}, u32[]{:S(2)}) collective-permute-start(bf16[128,1024]{1,0:T(8,128)(2,1)S(1)} %get-tuple-element.150), channel_id=1, source_target_pairs={{0,16},{4,20},{8,24},{12,28},{16,0},{20,4},{24,8},{28,12},{1,17},{... | collective-permute-start | bytes 786440 | tf_op jit(solution)/shard_map/ppermute | solution.py:285
  268.7 19.8 %collective-permute-start.64 = (bf16[128,1024]{1,0:T(8,128)(2,1)S(1)}, bf16[128,1024]{1,0:T(8,128)(2,1)S(1)}, u32[]{:S(2)}, u32[]{:S(2)}) collective-permute-start(bf16[128,1024]{1,0:T(8,128)(2,1)S(1)} %get-tuple-element.149), channel_id=1, source_target_pairs={{0,8},{4,12},{8,0},{12,4},{16,24},{20,28},{24,16},{28,20},{1,9},{5... | collective-permute-start | bytes 786440 | tf_op jit(solution)/shard_map/ppermute | solution.py:285
  268.9 19.6 %collective-permute-start.65 = (bf16[128,1024]{1,0:T(8,128)(2,1)S(1)}, bf16[128,1024]{1,0:T(8,128)(2,1)S(1)}, u32[]{:S(2)}, u32[]{:S(2)}) collective-permute-start(bf16[128,1024]{1,0:T(8,128)(2,1)S(1)} %get-tuple-element.148), channel_id=1, source_target_pairs={{0,24},{4,28},{8,16},{12,20},{16,8},{20,12},{24,0},{28,4},{1,25},{... | collective-permute-start | bytes 786440 | tf_op jit(solution)/shard_map/ppermute | solution.py:285
  282.4 27.6 %collective-permute-start.68 = (bf16[128,1024]{1,0:T(8,128)(2,1)}, bf16[128,1024]{1,0:T(8,128)(2,1)}, u32[]{:S(2)}, u32[]{:S(2)}) collective-permute-start(bf16[128,1024]{1,0:T(8,128)(2,1)} %get-tuple-element.146), channel_id=1, source_target_pairs={{0,8},{4,12},{8,0},{12,4},{16,24},{20,28},{24,16},{28,20},{1,9},{5... | collective-permute-start | bytes 786440 | tf_op jit(solution)/shard_map/ppermute | solution.py:285
  288.5 24.4 %collective-permute-start.69 = (bf16[128,1024]{1,0:T(8,128)(2,1)}, bf16[128,1024]{1,0:T(8,128)(2,1)}, u32[]{:S(2)}, u32[]{:S(2)}) collective-permute-start(bf16[128,1024]{1,0:T(8,128)(2,1)} %get-tuple-element.145), channel_id=1, source_target_pairs={{0,24},{4,28},{8,16},{12,20},{16,8},{20,12},{24,0},{28,4},{1,25},{... | collective-permute-start | bytes 786440 | tf_op jit(solution)/shard_map/ppermute | solution.py:285
  288.5 59.1 %collective-permute-start.57 = (bf16[512,1024]{1,0:T(8,128)(2,1)}, bf16[512,1024]{1,0:T(8,128)(2,1)}, u32[]{:S(2)}, u32[]{:S(2)}) collective-permute-start(bf16[512,1024]{1,0:T(8,128)(2,1)} %pad_maximum_fusion.5), channel_id=1, source_target_pairs={{0,4},{4,0},{8,12},{12,8},{16,20},{20,16},{24,28},{28,24},{1,5},{5... | collective-permute-start | bytes 3145736 | tf_op jit(solution)/shard_map/ppermute | solution.py:285
  297.2 5.8 %collective-permute-start.43 = (f32[5632]{0:T(1024)S(1)}, f32[5632]{0:T(1024)S(1)}, u32[]{:S(2)}, u32[]{:S(2)}) collective-permute-start(f32[5632]{0:T(1024)S(1)} %pad_maximum_fusion.24), channel_id=1, source_target_pairs={{0,2},{2,0},{1,3},{3,1},{4,6},{6,4},{5,7},{7,5},{8,10},{10,8},{9,1... | collective-permute-start | bytes 67592 | tf_op jit(solution)/shard_map/ppermute | solution.py:291
  303.1 51.7 %collective-permute-start.46 = (bf16[192,1024]{1,0:T(8,128)(2,1)}, bf16[192,1024]{1,0:T(8,128)(2,1)}, u32[]{:S(2)}, u32[]{:S(2)}) collective-permute-start(bf16[192,1024]{1,0:T(8,128)(2,1)} %slice.850), channel_id=1, source_target_pairs={{0,2},{2,0},{1,3},{3,1},{4,6},{6,4},{5,7},{7,5},{8,10},{10,8},{9,1... | collective-permute-start | bytes 1179656 | tf_op jit(solution)/shard_map/ppermute | solution.py:291
  306.2 12.6 %collective-permute-start.50 = (f32[1,7168]{1,0:T(1,128)S(1)}, f32[1,7168]{1,0:T(1,128)S(1)}, u32[]{:S(2)}, u32[]{:S(2)}) collective-permute-start(f32[1,7168]{1,0:T(1,128)S(1)} %bitcast.157), channel_id=1, source_target_pairs={{0,24},{4,28},{8,16},{12,20},{16,8},{20,12},{24,0},{28,4},{1,25},{... | collective-permute-start | bytes 86024 | tf_op jit(solution)/shard_map/ppermute | solution.py:285
  310.0 8.7 %collective-permute-start.49 = (f32[1,7168]{1,0:T(1,128)S(1)}, f32[1,7168]{1,0:T(1,128)S(1)}, u32[]{:S(2)}, u32[]{:S(2)}) collective-permute-start(f32[1,7168]{1,0:T(1,128)S(1)} %bitcast.158), channel_id=1, source_target_pairs={{0,8},{4,12},{8,0},{12,4},{16,24},{20,28},{24,16},{28,20},{1,9},{5... | collective-permute-start | bytes 86024 | tf_op jit(solution)/shard_map/ppermute | solution.py:285
  312.9 7.3 %collective-permute-start.48 = (f32[1,7168]{1,0:T(1,128)S(1)}, f32[1,7168]{1,0:T(1,128)S(1)}, u32[]{:S(2)}, u32[]{:S(2)}) collective-permute-start(f32[1,7168]{1,0:T(1,128)S(1)} %bitcast.159), channel_id=1, source_target_pairs={{0,16},{4,20},{8,24},{12,28},{16,0},{20,4},{24,8},{28,12},{1,17},{... | collective-permute-start | bytes 86024 | tf_op jit(solution)/shard_map/ppermute | solution.py:285
  318.7 58.2 %collective-permute-start.44 = (f32[1,192,1024]{2,1,0:T(8,128)}, f32[1,192,1024]{2,1,0:T(8,128)}, u32[]{:S(2)}, u32[]{:S(2)}) collective-permute-start(f32[1,192,1024]{2,1,0:T(8,128)} %get-tuple-element.196), channel_id=1, source_target_pairs={{0,1},{1,0},{2,3},{3,2},{4,5},{5,4},{6,7},{7,6},{8,9},{9,8},{10,11... | collective-permute-start | bytes 2359304 | tf_op jit(solution)/shard_map/ppermute | solution.py:294
  318.7 31.9 %collective-permute-start.70 = (bf16[64,2048]{1,0:T(8,128)(2,1)}, bf16[64,2048]{1,0:T(8,128)(2,1)}, u32[]{:S(2)}, u32[]{:S(2)}) collective-permute-start(bf16[64,2048]{1,0:T(8,128)(2,1)} %fusion.62), channel_id=1, source_target_pairs={{0,2},{2,0},{1,3},{3,1},{4,6},{6,4},{5,7},{7,5},{8,10},{10,8},{9,1... | collective-permute-start | bytes 786440 | tf_op jit(solution)/shard_map/ppermute | solution.py:291
  320.4 5.3 %collective-permute-start.51 = (f32[4,7168]{1,0:T(4,128)S(1)}, f32[4,7168]{1,0:T(4,128)S(1)}, u32[]{:S(2)}, u32[]{:S(2)}) collective-permute-start(f32[4,7168]{1,0:T(4,128)S(1)} %pad_maximum_fusion.22), channel_id=1, source_target_pairs={{0,4},{4,0},{8,12},{12,8},{16,20},{20,16},{24,28},{28,24},{1,5},{5... | collective-permute-start | bytes 344072 | tf_op jit(solution)/shard_map/ppermute | solution.py:285
  333.4 4.5 %collective-permute-start.54 = (f32[1,2,128]{2,0,1:T(1,128)S(1)}, f32[1,2,128]{2,0,1:T(1,128)S(1)}, u32[]{:S(2)}, u32[]{:S(2)}) collective-permute-start(f32[1,2,128]{2,0,1:T(1,128)S(1)} %get-tuple-element.186), channel_id=1, source_target_pairs={{0,16},{4,20},{8,24},{12,28},{16,0},{20,4},{24,8},{28,12},{1,17},{... | collective-permute-start | bytes 3080 | tf_op jit(solution)/shard_map/ppermute | solution.py:285
  341.6 5.4 %collective-permute-start.56 = (f32[1,2,128]{2,0,1:T(1,128)S(1)}, f32[1,2,128]{2,0,1:T(1,128)S(1)}, u32[]{:S(2)}, u32[]{:S(2)}) collective-permute-start(f32[1,2,128]{2,0,1:T(1,128)S(1)} %get-tuple-element.184), channel_id=1, source_target_pairs={{0,24},{4,28},{8,16},{12,20},{16,8},{20,12},{24,0},{28,4},{1,25},{... | collective-permute-start | bytes 3080 | tf_op jit(solution)/shard_map/ppermute | solution.py:285
  349.2 12.1 %collective-permute-start.60 = (bf16[128,1024]{1,0:T(8,128)(2,1)S(1)}, bf16[128,1024]{1,0:T(8,128)(2,1)S(1)}, u32[]{:S(2)}, u32[]{:S(2)}) collective-permute-start(bf16[128,1024]{1,0:T(8,128)(2,1)S(1)} %get-tuple-element.152), channel_id=1, source_target_pairs={{0,24},{4,28},{8,16},{12,20},{16,8},{20,12},{24,0},{28,4},{1,25},{... | collective-permute-start | bytes 786440 | tf_op jit(solution)/shard_map/ppermute | solution.py:285
  350.7 11.2 %collective-permute-start.59 = (bf16[128,1024]{1,0:T(8,128)(2,1)S(1)}, bf16[128,1024]{1,0:T(8,128)(2,1)S(1)}, u32[]{:S(2)}, u32[]{:S(2)}) collective-permute-start(bf16[128,1024]{1,0:T(8,128)(2,1)S(1)} %get-tuple-element.153), channel_id=1, source_target_pairs={{0,8},{4,12},{8,0},{12,4},{16,24},{20,28},{24,16},{28,20},{1,9},{5... | collective-permute-start | bytes 786440 | tf_op jit(solution)/shard_map/ppermute | solution.py:285
  350.7 19.1 %collective-permute-start.58 = (bf16[128,1024]{1,0:T(8,128)(2,1)S(1)}, bf16[128,1024]{1,0:T(8,128)(2,1)S(1)}, u32[]{:S(2)}, u32[]{:S(2)}) collective-permute-start(bf16[128,1024]{1,0:T(8,128)(2,1)S(1)} %get-tuple-element.151), channel_id=1, source_target_pairs={{0,16},{4,20},{8,24},{12,28},{16,0},{20,4},{24,8},{28,12},{1,17},{... | collective-permute-start | bytes 786440 | tf_op jit(solution)/shard_map/ppermute | solution.py:285
  361.3 17.0 %collective-permute-start.47 = (f32[1,192,1024]{2,1,0:T(8,128)S(1)}, f32[1,192,1024]{2,1,0:T(8,128)S(1)}, u32[]{:S(2)}, u32[]{:S(2)}) collective-permute-start(f32[1,192,1024]{2,1,0:T(8,128)S(1)} %get-tuple-element.198), channel_id=1, source_target_pairs={{0,1},{1,0},{2,3},{3,2},{4,5},{5,4},{6,7},{7,6},{8,9},{9,8},{10,11... | collective-permute-start | bytes 2359304 | tf_op jit(solution)/shard_map/ppermute | solution.py:294
  371.1 5.0 %collective-permute-start.61 = (bf16[64,1024]{1,0:T(8,128)(2,1)S(1)}, bf16[64,1024]{1,0:T(8,128)(2,1)S(1)}, u32[]{:S(2)}, u32[]{:S(2)}) collective-permute-start(bf16[64,1024]{1,0:T(8,128)(2,1)S(1)} %dynamic-slice_convert_fusion), channel_id=1, source_target_pairs={{0,2},{2,0},{1,3},{3,1},{4,6},{6,4},{5,7},{7,5},{8,10},{10,8},{9,1... | collective-permute-start | bytes 393224 | tf_op jit(solution)/shard_map/ppermute | solution.py:291
  (110 other events, 1078.5 us)
where the time goes:
time: 387 us; the launch traced here: 380 us
  waiting for transfers between devices  135 us (35%)
  starting transfers between devices  91.4 us (24%)
  matrix products  62.2 us (16%)
  other arithmetic  41.3 us (11%)
  Pallas kernels  31.2 us (8%)
  local copies, waits for them, and re-layouts  16.2 us (4%)
    ppermute x47, waiting for transfers between devices, swap(): return lax.ppermute(v, 'shard', [(s, s ^ mask) for s in range(shards)])  104 us
    ppermute x47, starting transfers between devices, swap(): return lax.ppermute(v, 'shard', [(s, s ^ mask) for s in range(shards)])  77.2 us
    dot_general x33, matrix products, dot(): lax.dot_general(a, b, ((contract[:1], contract[1:]), ((), ())), preferred...  62.2 us
    ppermute x11, waiting for transfers between devices, from_ctx(): return lax.ppermute(v, 'ctx', [(i, (i - k) % ctxs) for i in range(ctxs)])  30.7 us
    ppermute x11, starting transfers between devices, from_ctx(): return lax.ppermute(v, 'ctx', [(i, (i - k) % ctxs) for i in range(ctxs)])  13.2 us
    pallas_call x1, Pallas kernels, attend(): pl.pallas_call(lambda *refs: attend_kernel(_chunk(rows), *refs), grid=(st...  11.2 us
    pallas_call x1, Pallas kernels, attend_back(): pl.pallas_call(lambda *refs: attend_back_kernel(_chunk(rows), steps, *ref...  10.7 us
  transfers between devices with their start and end apart: 71, of which 27 were waited for; matrix products, arithmetic and copies ran while one was open for 26% of the time, Pallas kernels for 7%

commit v1 on v0

--- a/solution.py
+++ b/solution.py
@@ -5,6 +5,7 @@
 from jax.experimental.pallas import tpu as pltpu
 from jax.sharding import PartitionSpec as P
 
+SHARD, CTX, TENSOR = "shard", "ctx", "tensor"
 HD = 64
 EPS = 1e-06
 f32 = jnp.float32
@@ -93,7 +94,7 @@
     rows, columns = pairs[0].shape
     return pl.pallas_call(
         assemble_kernel,
-        out_shape=jax.ShapeDtypeStruct((rows * len(pairs), columns), bf16),
+        out_shape=pltpu.VMEM((rows * len(pairs), columns), bf16),
         cost_estimate=_CHEAP,
         name="assemble",
     )(*pairs)
@@ -262,12 +263,12 @@
     cotangent,
 ):
     latents, own_rows, width = tokens.shape
-    shards = lax.axis_size("shard")
-    ctxs = lax.axis_size("ctx")
-    tens = lax.axis_size("tensor")
-    shard_at = lax.axis_index("shard")
-    ctx_at = lax.axis_index("ctx")
-    tensor_at = lax.axis_index("tensor")
+    shards = lax.axis_size(SHARD)
+    ctxs = lax.axis_size(CTX)
+    tens = lax.axis_size(TENSOR)
+    shard_at = lax.axis_index(SHARD)
+    ctx_at = lax.axis_index(CTX)
+    tensor_at = lax.axis_index(TENSOR)
     blk = width // shards
     share = own_rows // tens
     cols_c = qkv_weight.shape[2]
@@ -282,16 +283,16 @@
         return sum(((place >> i) & 1) << (bits - 1 - i) for i in range(bits))
 
     def swap(v, mask):
-        return lax.ppermute(v, "shard", [(s, s ^ mask) for s in range(shards)])
+        return lax.ppermute(v, SHARD, [(s, s ^ mask) for s in range(shards)])
 
     def tie(v, *after):
         return lax.optimization_barrier((v, *after))[0]
 
     def from_ctx(v, k):
-        return lax.ppermute(v, "ctx", [(i, (i - k) % ctxs) for i in range(ctxs)])
+        return lax.ppermute(v, CTX, [(i, (i - k) % ctxs) for i in range(ctxs)])
 
     def from_core(v, k):
-        return lax.ppermute(v, "tensor", [(i, (i - k) % tens) for i in range(tens)])
+        return lax.ppermute(v, TENSOR, [(i, (i - k) % tens) for i in range(tens)])
 
     def gather_half(piece):
         parts = [piece]
@@ -637,33 +638,33 @@
 
 def solution(mesh):
     in_specs = (
-        P("shard", "ctx", None),
-        P("shard", None),
-        P("shard", None, "tensor"),
-        P(None, "tensor"),
-        P("shard", None, "tensor"),
-        P(None, "tensor"),
-        P("tensor", "shard"),
+        P(SHARD, CTX, None),
+        P(SHARD, None),
+        P(SHARD, None, TENSOR),
+        P(None, TENSOR),
+        P(SHARD, None, TENSOR),
+        P(None, TENSOR),
+        P(TENSOR, SHARD),
         P(),
-        P("shard", "tensor"),
-        P("tensor"),
-        P("tensor", "shard"),
+        P(SHARD, TENSOR),
+        P(TENSOR),
+        P(TENSOR, SHARD),
         P(),
-        P("shard", "ctx", None),
+        P(SHARD, CTX, None),
     )
     out_specs = (
-        P("shard", "ctx", None),
-        P("shard", "ctx", None),
-        P("shard", None),
-        P(("shard", "ctx"), None, "tensor"),
-        P(None, "tensor"),
-        P(("shard", "ctx"), None, "tensor"),
-        P(None, "tensor"),
-        P("tensor", ("shard", "ctx")),
+        P(SHARD, CTX, None),
+        P(SHARD, CTX, None),
+        P(SHARD, None),
+        P((SHARD, CTX), None, TENSOR),
+        P(None, TENSOR),
+        P((SHARD, CTX), None, TENSOR),
+        P(None, TENSOR),
+        P(TENSOR, (SHARD, CTX)),
         P(),
-        P(("shard", "ctx"), "tensor"),
-        P("tensor"),
-        P("tensor", ("shard", "ctx")),
+        P((SHARD, CTX), TENSOR),
+        P(TENSOR),
+        P(TENSOR, (SHARD, CTX)),
         P(),
     )
     return jax.shard_map(layer, mesh=mesh, in_specs=in_specs, out_specs=out_specs, check_vma=False)

time: 387 us -> 386 us (level)
  transfers between devices with their start and end apart: 71 -> 71, of which waited for: 27 -> 28; matrix products, arithmetic and copies ran while one was open for 26% -> 26% of each run, Pallas kernels for 7% -> 7%
where the time goes in v1:
time: 386 us; the launch traced here: 379 us
  waiting for transfers between devices  135 us (35%)
  starting transfers between devices  92.7 us (24%)
  matrix products  59.2 us (15%)
  other arithmetic  40.7 us (11%)
  Pallas kernels  29.7 us (8%)
  local copies, waits for them, and re-layouts  18.6 us (5%)
    ppermute x47, waiting for transfers between devices, swap(): return lax.ppermute(v, SHARD, [(s, s ^ mask) for s in range(shards)])  104 us
    ppermute x47, starting transfers between devices, swap(): return lax.ppermute(v, SHARD, [(s, s ^ mask) for s in range(shards)])  77.9 us
    dot_general x33, matrix products, dot(): lax.dot_general(a, b, ((contract[:1], contract[1:]), ((), ())), preferred...  59.2 us
    ppermute x11, waiting for transfers between devices, from_ctx(): return lax.ppermute(v, CTX, [(i, (i - k) % ctxs) for i in range(ctxs)])  31.5 us
    ppermute x11, starting transfers between devices, from_ctx(): return lax.ppermute(v, CTX, [(i, (i - k) % ctxs) for i in range(ctxs)])  13.7 us
    pallas_call x1, Pallas kernels, attend(): pl.pallas_call(lambda *refs: attend_kernel(_chunk(rows), *refs), grid=(st...  11.2 us
    pallas_call x1, Pallas kernels, attend_back(): pl.pallas_call(lambda *refs: attend_back_kernel(_chunk(rows), steps, *ref...  10.5 us
  transfers between devices with their start and end apart: 71, of which 28 were waited for; matrix products, arithmetic and copies ran while one was open for 26% of the time, Pallas kernels for 7%

profile of v1, /device:TPU:0, one launch (start us, length us, event | category | flops | bytes accessed | tf_op | source)
XLA Modules:
  0.0 379.1 jit_solution(8410648938251216739)
XLA Ops:
  0.7 5.1 %collective-permute-start.2 = (bf16[1,1024]{1,0:T(2,128)(2,1)}, bf16[1,1024]{1,0:T(2,128)(2,1)S(1)}, u32[]{:S(2)}, u32[]{:S(2)}) collective-permute-start(bf16[1,1024]{1,0:T(2,128)(2,1)} %param.14), channel_id=1, source_target_pairs={{0,24},{4,28},{8,16},{12,20},{16,8},{20,12},{24,0},{28,4},{1,25},{... | collective-permute-start | bytes 6152 | tf_op jit(solution)/shard_map/ppermute | solution.py:286
  7.7 1.7 collective-permute-start.9
  9.8 2.2 collective-permute-start.11
  14.0 1.7 collective-permute-done.3
  18.0 2.6 collective-permute-done.4
  22.8 2.3 collective-permute-start.5
  31.7 3.0 fusion.3
  43.8 1.9 collective-permute-done.14.refs_8_
  46.0 3.9 %collective-permute-done.15.refs_9_ = bf16[128,768]{1,0:T(8,128)(2,1)S(1)} collective-permute-done((bf16[128,768]{1,0:T(8,128)(2,1)S(1)}, bf16[128,768]{1,0:T(8,128)(2,1)S(1)}, u32[]{:S(2)}, u32[]{:S(2)}) %collective-permute-start.15) | collective-permute-done | bytes 196640 | tf_op jit(solution)/shard_map/ppermute | solution.py:286
  49.9 2.4 collective-permute-start.20
  52.3 2.4 pad_maximum_fusion.1.refs_0_
  54.7 3.0 collective-permute-done.17.refs_11_
  58.4 6.3 %project.1 = (bf16[768,768]{1,0:T(8,128)(2,1)}, bf16[768,1024]{1,0:T(8,128)(2,1)}, bf16[1024,768]{1,0:T(8,128)(2,1)}) custom-call(bf16[768,1024]{1,0:T(8,128)(2,1)} %pad_maximum_fusion.1.refs_0_, f32[1,1024]{1,0:T(1,128)} %get-tuple-element.174.refs_1_, f32[1,1024]{1,0:T(1,128)} %get-tuple-element.173.refs_2_, f32[1,768]{1,0:T(1,128)} %broadcast_in_dim.54.refs_3_, ...), custom_call_target="tpu_custom_call" | custom-call | flops 1000 | bytes 1000 | tf_op jit(solution)/shard_map/project/pallas_call | solution.py:106
  66.4 11.2 %attend.1 = (bf16[768,256]{1,0:T(8,128)(2,1)}, f32[16,768]{1,0:T(8,128)}) custom-call(bf16[768,768]{1,0:T(8,128)(2,1)} %get-tuple-element.52.refs_0_.refs_1_.refs_2_, bf16[768,768]{1,0:T(8,128)(2,1)} %get-tuple-element.52.refs_0_.refs_1_.refs_2_, bf16[768,768]{1,0:T(8,128)(2,1)} %get-tuple-element.52.refs_0_.refs_1_.refs_2_), custom_call_target="tpu_custom_call" | custom-call | flops 1000 | bytes 1000 | tf_op jit(solution)/shard_map/attend/pallas_call | solution.py:209
  77.6 2.3 convolution_convert_fusion.3
  80.3 2.5 collective-permute-start.27
  84.4 2.7 convolution_convert_fusion.7
  88.1 1.6 collective-permute-start.23
  91.7 3.5 collective-permute-done.26
  95.2 5.6 %collective-permute-done.27 = bf16[128,1024]{1,0:T(8,128)(2,1)S(1)} collective-permute-done((bf16[128,1024]{1,0:T(8,128)(2,1)S(1)}, bf16[128,1024]{1,0:T(8,128)(2,1)S(1)}, u32[]{:S(2)}, u32[]{:S(2)}) %collective-permute-start.27) | collective-permute-done | bytes 262176 | tf_op jit(solution)/shard_map/ppermute | solution.py:286
  100.8 5.5 %collective-permute-done.23 = bf16[192,1024]{1,0:T(8,128)(2,1)S(1)} collective-permute-done((bf16[192,1024]{1,0:T(8,128)(2,1)S(1)}, bf16[192,1024]{1,0:T(8,128)(2,1)S(1)}, u32[]{:S(2)}, u32[]{:S(2)}) %collective-permute-start.23) | collective-permute-done | bytes 393248 | tf_op jit(solution)/shard_map/ppermute | solution.py:292
  110.8 6.7 %collective-permute-done.24 = bf16[192,1024]{1,0:T(8,128)(2,1)S(1)} collective-permute-done((bf16[192,1024]{1,0:T(8,128)(2,1)S(1)}, bf16[192,1024]{1,0:T(8,128)(2,1)S(1)}, u32[]{:S(2)}, u32[]{:S(2)}) %collective-permute-start.24) | collective-permute-done | bytes 393248 | tf_op jit(solution)/shard_map/ppermute | solution.py:292
  119.4 22.2 %collective-permute-done.32 = bf16[128,1024]{1,0:T(8,128)(2,1)S(1)} collective-permute-done((bf16[128,1024]{1,0:T(8,128)(2,1)S(1)}, bf16[128,1024]{1,0:T(8,128)(2,1)S(1)}, u32[]{:S(2)}, u32[]{:S(2)}) %collective-permute-start.32) | collective-permute-done | bytes 262176 | tf_op jit(solution)/shard_map/ppermute | solution.py:286
  143.3 2.3 collective-permute-start.34
  148.6 6.4 %multiply_convert_fusion.1 = (bf16[768,1024]{1,0:T(8,128)(2,1)S(1)}, f32[768,1024]{1,0:T(8,128)}) fusion(f32[1024]{0:T(1024)S(1)} %dynamic_slice.48, bf16[512,1024]{1,0:T(8,128)(2,1)} %collective-permute-done.29, bf16[512,1024]{1,0:T(8,128)(2,1)} %pad_maximum_fusion.4, bf16[384,1024]{1,0:T(8,128)(2,1)} %collective-permute-done.25, ...), kind=kOutput, calls=%fused_computation.41 | convolution fusion | flops 1627389952 | bytes 8392704 | tf_op jit(solution)/shard_map/dot_general | solution.py:43
  155.0 14.6 %collective-permute-done.33.refs_1_ = bf16[256,1024]{1,0:T(8,128)(2,1)S(1)} collective-permute-done((bf16[256,1024]{1,0:T(8,128)(2,1)S(1)}, bf16[256,1024]{1,0:T(8,128)(2,1)S(1)}, u32[]{:S(2)}, u32[]{:S(2)}) %collective-permute-start.33) | collective-permute-done | bytes 524320 | tf_op jit(solution)/shard_map/ppermute | solution.py:286
  169.7 9.9 %collective-permute-done.35.refs_3_ = bf16[256,1024]{1,0:T(8,128)(2,1)S(1)} collective-permute-done((bf16[256,1024]{1,0:T(8,128)(2,1)S(1)}, bf16[256,1024]{1,0:T(8,128)(2,1)S(1)}, u32[]{:S(2)}, u32[]{:S(2)}) %collective-permute-start.35) | collective-permute-done | bytes 524320 | tf_op jit(solution)/shard_map/ppermute | solution.py:286
  180.4 2.0 convolution_convert_fusion.1
  182.4 1.7 assemble.1
  184.1 6.5 %fusion.159 = (f32[1024]{0:T(1024)}, bf16[768,1024]{1,0:T(8,128)(2,1)S(1)}) fusion(f32[768,1024]{1,0:T(8,128)} %get-tuple-element.192, f32[1024]{0:T(1024)S(1)} %dynamic_slice.48, bf16[768,1024]{1,0:T(8,128)(2,1)} %copy-done.20, bf16[1024,1024]{1,0:T(8,128)(2,1)S(1)} %assemble.1), kind=kOutput, calls=%fused_computation.342 | convolution fusion | flops 1627913216 | bytes 8396800 | tf_op jit(solution)/shard_map/dot_general | solution.py:43
  190.6 4.0 %convolution_convert_fusion.5 = bf16[384,1024]{1,0:T(8,128)(2,1)} fusion(bf16[768,1024]{1,0:T(8,128)(2,1)S(1)} %get-tuple-element.80, bf16[512,1024]{1,0:T(8,128)(2,1)} %collective-permute-done.29, bf16[512,1024]{1,0:T(8,128)(2,1)} %pad_maximum_fusion.4), kind=kOutput, calls=%fused_computation.58 | convolution fusion | flops 809893888 | bytes 3670016 | tf_op jit(solution)/shard_map/dot_general | solution.py:43
  197.2 2.9 convert_add_fusion.2
  204.6 2.4 fusion.32
  207.0 7.1 %collective-permute-done.39 = bf16[192,1024]{1,0:T(8,128)(2,1)S(1)} collective-permute-done((bf16[192,1024]{1,0:T(8,128)(2,1)S(1)}, bf16[192,1024]{1,0:T(8,128)(2,1)S(1)}, u32[]{:S(2)}, u32[]{:S(2)}) %collective-permute-start.39) | collective-permute-done | bytes 393248 | tf_op jit(solution)/shard_map/ppermute | solution.py:292
  218.6 8.4 %collective-permute-done.40 = bf16[192,1024]{1,0:T(8,128)(2,1)S(1)} collective-permute-done((bf16[192,1024]{1,0:T(8,128)(2,1)S(1)}, bf16[192,1024]{1,0:T(8,128)(2,1)S(1)}, u32[]{:S(2)}, u32[]{:S(2)}) %collective-permute-start.40) | collective-permute-done | bytes 393248 | tf_op jit(solution)/shard_map/ppermute | solution.py:292
  227.1 2.0 convolution_convert_fusion
  231.8 11.8 %collective-permute-start.67 = (bf16[128,1024]{1,0:T(8,128)(2,1)}, bf16[128,1024]{1,0:T(8,128)(2,1)}, u32[]{:S(2)}, u32[]{:S(2)}) collective-permute-start(bf16[128,1024]{1,0:T(8,128)(2,1)} %get-tuple-element.147), channel_id=1, source_target_pairs={{0,16},{4,20},{8,24},{12,28},{16,0},{20,4},{24,8},{28,12},{1,17},{... | collective-permute-start | bytes 786440 | tf_op jit(solution)/shard_map/ppermute | solution.py:286
  249.6 10.5 %attend_back.1 = (bf16[768,768]{1,0:T(8,128)(2,1)}, f32[16,128]{1,0:T(8,128)}) custom-call(bf16[768,768]{1,0:T(8,128)(2,1)} %get-tuple-element.52.refs_0_.refs_1_.refs_2_, bf16[768,768]{1,0:T(8,128)(2,1)} %get-tuple-element.52.refs_0_.refs_1_.refs_2_, bf16[768,768]{1,0:T(8,128)(2,1)} %get-tuple-element.52.refs_0_.refs_1_.refs_2_, ...), custom_call_target="tpu_custom_call" | custom-call | flops 1000 | bytes 1000 | tf_op jit(solution)/shard_map/attend_back/pallas_call | solution.py:230
  260.1 2.5 convolution_convert_fusion.2
  268.3 1.6 collective-permute-start.64
  269.9 1.6 collective-permute-start.65
  271.5 2.2 fusion.27
  274.9 8.5 %collective-permute-done.63 = bf16[128,1024]{1,0:T(8,128)(2,1)S(1)} collective-permute-done((bf16[128,1024]{1,0:T(8,128)(2,1)S(1)}, bf16[128,1024]{1,0:T(8,128)(2,1)S(1)}, u32[]{:S(2)}, u32[]{:S(2)}) %collective-permute-start.63) | collective-permute-done | bytes 262176 | tf_op jit(solution)/shard_map/ppermute | solution.py:286
  283.4 3.4 collective-permute-done.64
  286.8 1.9 collective-permute-start.69
  291.4 2.3 fusion.15
  293.7 1.7 fusion.112
  298.5 2.0 fusion.43
  304.8 1.7 collective-permute-start.50
  306.5 4.8 %collective-permute-start.49 = (f32[1,7168]{1,0:T(1,128)S(1)}, f32[1,7168]{1,0:T(1,128)S(1)}, u32[]{:S(2)}, u32[]{:S(2)}) collective-permute-start(f32[1,7168]{1,0:T(1,128)S(1)} %bitcast.158), channel_id=1, source_target_pairs={{0,8},{4,12},{8,0},{12,4},{16,24},{20,28},{24,16},{28,20},{1,9},{5... | collective-permute-start | bytes 86024 | tf_op jit(solution)/shard_map/ppermute | solution.py:286
  311.9 2.0 constant_dynamic-update-slice_fusion.13
  313.9 2.1 fusion.80
  319.3 4.2 %collective-permute-done.51 = f32[4,7168]{1,0:T(4,128)S(1)} collective-permute-done((f32[4,7168]{1,0:T(4,128)S(1)}, f32[4,7168]{1,0:T(4,128)S(1)}, u32[]{:S(2)}, u32[]{:S(2)}) %collective-permute-start.51) | collective-permute-done | bytes 114720 | tf_op jit(solution)/shard_map/ppermute | solution.py:286
  329.9 2.0 collective-permute-done.53
  331.9 2.8 collective-permute-start.54
  334.7 2.0 collective-permute-done.54
  336.6 2.0 collective-permute-start.55
  340.2 2.0 collective-permute-start.56
  342.2 3.3 collective-permute-done.56
  346.2 1.8 fusion.74
  348.0 2.1 collective-permute-start.60
  350.8 2.4 collective-permute-start.58
  361.8 6.8 %collective-permute-done.58 = bf16[128,1024]{1,0:T(8,128)(2,1)S(1)} collective-permute-done((bf16[128,1024]{1,0:T(8,128)(2,1)S(1)}, bf16[128,1024]{1,0:T(8,128)(2,1)S(1)}, u32[]{:S(2)}, u32[]{:S(2)}) %collective-permute-start.58) | collective-permute-done | bytes 262176 | tf_op jit(solution)/shard_map/ppermute | solution.py:286
  371.1 3.8 %collective-permute-done.61 = bf16[64,1024]{1,0:T(8,128)(2,1)S(1)} collective-permute-done((bf16[64,1024]{1,0:T(8,128)(2,1)S(1)}, bf16[64,1024]{1,0:T(8,128)(2,1)S(1)}, u32[]{:S(2)}, u32[]{:S(2)}) %collective-permute-start.61) | collective-permute-done | bytes 131104 | tf_op jit(solution)/shard_map/ppermute | solution.py:292
  (491 shorter events, 108.1 us)
Async XLA Ops:
  0.7 11.3 %collective-permute-start.2 = (bf16[1,1024]{1,0:T(2,128)(2,1)}, bf16[1,1024]{1,0:T(2,128)(2,1)S(1)}, u32[]{:S(2)}, u32[]{:S(2)}) collective-permute-start(bf16[1,1024]{1,0:T(2,128)(2,1)} %param.14), channel_id=1, source_target_pairs={{0,24},{4,28},{8,16},{12,20},{16,8},{20,12},{24,0},{28,4},{1,25},{... | collective-permute-start | bytes 6152 | tf_op jit(solution)/shard_map/ppermute | solution.py:286
  5.8 6.2 %collective-permute-start.1 = (bf16[1,1024]{1,0:T(2,128)(2,1)}, bf16[1,1024]{1,0:T(2,128)(2,1)S(1)}, u32[]{:S(2)}, u32[]{:S(2)}) collective-permute-start(bf16[1,1024]{1,0:T(2,128)(2,1)} %param.14), channel_id=1, source_target_pairs={{0,8},{4,12},{8,0},{12,4},{16,24},{20,28},{24,16},{28,20},{1,9},{5... | collective-permute-start | bytes 6152 | tf_op jit(solution)/shard_map/ppermute | solution.py:286
  5.8 6.2 %collective-permute-start = (bf16[1,1024]{1,0:T(2,128)(2,1)}, bf16[1,1024]{1,0:T(2,128)(2,1)S(1)}, u32[]{:S(2)}, u32[]{:S(2)}) collective-permute-start(bf16[1,1024]{1,0:T(2,128)(2,1)} %param.14), channel_id=1, source_target_pairs={{0,16},{4,20},{8,24},{12,28},{16,0},{20,4},{24,8},{28,12},{1,17},{... | collective-permute-start | bytes 6152 | tf_op jit(solution)/shard_map/ppermute | solution.py:286
  7.7 23.0 %collective-permute-start.9 = (bf16[192,1024]{1,0:T(8,128)(2,1)S(1)}, bf16[192,1024]{1,0:T(8,128)(2,1)S(1)}, u32[]{:S(2)}, u32[]{:S(2)}) collective-permute-start(bf16[192,1024]{1,0:T(8,128)(2,1)S(1)} %convolution_convert_fusion.8), channel_id=1, source_target_pairs={{0,2},{2,0},{1,3},{3,1},{4,6},{6,4},{5,7},{7,5},{8,10},{10,8},{9,1... | collective-permute-start | bytes 1179656 | tf_op jit(solution)/shard_map/ppermute | solution.py:292
  9.8 30.8 %collective-permute-start.11 = (bf16[128,768]{1,0:T(8,128)(2,1)S(1)}, bf16[128,768]{1,0:T(8,128)(2,1)S(1)}, u32[]{:S(2)}, u32[]{:S(2)}) collective-permute-start(bf16[128,768]{1,0:T(8,128)(2,1)S(1)} %copy.48.refs_4_), channel_id=1, source_target_pairs={{0,16},{4,20},{8,24},{12,28},{16,0},{20,4},{24,8},{28,12},{1,17},{... | collective-permute-start | bytes 589832 | tf_op jit(solution)/shard_map/ppermute | solution.py:286
  20.6 5.7 %collective-permute-start.7 = (f32[1,3072]{1,0:T(1,128)S(1)}, f32[1,3072]{1,0:T(1,128)S(1)}, u32[]{:S(2)}, u32[]{:S(2)}) collective-permute-start(f32[1,3072]{1,0:T(1,128)S(1)} %get-tuple-element.167), channel_id=1, source_target_pairs={{0,24},{4,28},{8,16},{12,20},{16,8},{20,12},{24,0},{28,4},{1,25},{... | collective-permute-start | bytes 36872 | tf_op jit(solution)/shard_map/ppermute | solution.py:286
  22.2 4.6 %collective-permute-start.6 = (f32[1,3072]{1,0:T(1,128)S(1)}, f32[1,3072]{1,0:T(1,128)S(1)}, u32[]{:S(2)}, u32[]{:S(2)}) collective-permute-start(f32[1,3072]{1,0:T(1,128)S(1)} %get-tuple-element.168), channel_id=1, source_target_pairs={{0,8},{4,12},{8,0},{12,4},{16,24},{20,28},{24,16},{28,20},{1,9},{5... | collective-permute-start | bytes 36872 | tf_op jit(solution)/shard_map/ppermute | solution.py:286
  22.8 6.7 %collective-permute-start.5 = (f32[1,3072]{1,0:T(1,128)S(1)}, f32[1,3072]{1,0:T(1,128)S(1)}, u32[]{:S(2)}, u32[]{:S(2)}) collective-permute-start(f32[1,3072]{1,0:T(1,128)S(1)} %get-tuple-element.166), channel_id=1, source_target_pairs={{0,16},{4,20},{8,24},{12,28},{16,0},{20,4},{24,8},{28,12},{1,17},{... | collective-permute-start | bytes 36872 | tf_op jit(solution)/shard_map/ppermute | solution.py:286
  26.3 14.9 %collective-permute-start.12 = (bf16[128,768]{1,0:T(8,128)(2,1)S(1)}, bf16[128,768]{1,0:T(8,128)(2,1)S(1)}, u32[]{:S(2)}, u32[]{:S(2)}) collective-permute-start(bf16[128,768]{1,0:T(8,128)(2,1)S(1)} %copy.48.refs_4_), channel_id=1, source_target_pairs={{0,8},{4,12},{8,0},{12,4},{16,24},{20,28},{24,16},{28,20},{1,9},{5... | collective-permute-start | bytes 589832 | tf_op jit(solution)/shard_map/ppermute | solution.py:286
  26.8 15.9 %collective-permute-start.13 = (bf16[128,768]{1,0:T(8,128)(2,1)S(1)}, bf16[128,768]{1,0:T(8,128)(2,1)S(1)}, u32[]{:S(2)}, u32[]{:S(2)}) collective-permute-start(bf16[128,768]{1,0:T(8,128)(2,1)S(1)} %copy.48.refs_4_), channel_id=1, source_target_pairs={{0,24},{4,28},{8,16},{12,20},{16,8},{20,12},{24,0},{28,4},{1,25},{... | collective-permute-start | bytes 589832 | tf_op jit(solution)/shard_map/ppermute | solution.py:286
  31.7 18.2 %collective-permute-start.10 = (bf16[384,1024]{1,0:T(8,128)(2,1)}, bf16[384,1024]{1,0:T(8,128)(2,1)}, u32[]{:S(2)}, u32[]{:S(2)}) collective-permute-start(bf16[384,1024]{1,0:T(8,128)(2,1)} %pad_maximum_fusion.6), channel_id=1, source_target_pairs={{0,1},{1,0},{2,3},{3,2},{4,5},{5,4},{6,7},{7,6},{8,9},{9,8},{10,11... | collective-permute-start | bytes 2359304 | tf_op jit(solution)/shard_map/ppermute | solution.py:295
  37.9 7.8 %collective-permute-start.14 = (bf16[128,768]{1,0:T(8,128)(2,1)S(1)}, bf16[128,768]{1,0:T(8,128)(2,1)S(1)}, u32[]{:S(2)}, u32[]{:S(2)}) collective-permute-start(bf16[128,768]{1,0:T(8,128)(2,1)S(1)} %copy.48.refs_4_), channel_id=1, source_target_pairs={{0,4},{4,0},{8,12},{12,8},{16,20},{20,16},{24,28},{28,24},{1,5},{5... | collective-permute-start | bytes 589832 | tf_op jit(solution)/shard_map/ppermute | solution.py:286
  40.6 9.3 %collective-permute-start.15 = (bf16[128,768]{1,0:T(8,128)(2,1)S(1)}, bf16[128,768]{1,0:T(8,128)(2,1)S(1)}, u32[]{:S(2)}, u32[]{:S(2)}) collective-permute-start(bf16[128,768]{1,0:T(8,128)(2,1)S(1)} %collective-permute-done.11.refs_5_), channel_id=1, source_target_pairs={{0,4},{4,0},{8,12},{12,8},{16,20},{20,16},{24,28},{28,24},{1,5},{5... | collective-permute-start | bytes 589832 | tf_op jit(solution)/shard_map/ppermute | solution.py:286
  41.2 13.5 %collective-permute-start.16 = (bf16[128,768]{1,0:T(8,128)(2,1)S(1)}, bf16[128,768]{1,0:T(8,128)(2,1)S(1)}, u32[]{:S(2)}, u32[]{:S(2)}) collective-permute-start(bf16[128,768]{1,0:T(8,128)(2,1)S(1)} %collective-permute-done.12.refs_6_), channel_id=1, source_target_pairs={{0,4},{4,0},{8,12},{12,8},{16,20},{20,16},{24,28},{28,24},{1,5},{5... | collective-permute-start | bytes 589832 | tf_op jit(solution)/shard_map/ppermute | solution.py:286
  42.7 15.0 %collective-permute-start.17 = (bf16[128,768]{1,0:T(8,128)(2,1)S(1)}, bf16[128,768]{1,0:T(8,128)(2,1)S(1)}, u32[]{:S(2)}, u32[]{:S(2)}) collective-permute-start(bf16[128,768]{1,0:T(8,128)(2,1)S(1)} %collective-permute-done.13.refs_7_), channel_id=1, source_target_pairs={{0,4},{4,0},{8,12},{12,8},{16,20},{20,16},{24,28},{28,24},{1,5},{5... | collective-permute-start | bytes 589832 | tf_op jit(solution)/shard_map/ppermute | solution.py:286
  45.7 19.0 %collective-permute-start.18 = (bf16[128,256]{0,1:T(8,128)(2,1)S(1)}, bf16[128,256]{0,1:T(8,128)(2,1)S(1)}, u32[]{:S(2)}, u32[]{:S(2)}) collective-permute-start(bf16[128,256]{0,1:T(8,128)(2,1)S(1)} %dynamic-slice_bitcast_fusion.3), channel_id=1, source_target_pairs={{0,16},{4,20},{8,24},{12,28},{16,0},{20,4},{24,8},{28,12},{1,17},{... | collective-permute-start | bytes 196616 | tf_op jit(solution)/shard_map/ppermute | solution.py:286
  49.9 14.8 %collective-permute-start.19 = (bf16[128,256]{0,1:T(8,128)(2,1)S(1)}, bf16[128,256]{0,1:T(8,128)(2,1)S(1)}, u32[]{:S(2)}, u32[]{:S(2)}) collective-permute-start(bf16[128,256]{0,1:T(8,128)(2,1)S(1)} %dynamic-slice_bitcast_fusion.3), channel_id=1, source_target_pairs={{0,8},{4,12},{8,0},{12,4},{16,24},{20,28},{24,16},{28,20},{1,9},{5... | collective-permute-start | bytes 196616 | tf_op jit(solution)/shard_map/ppermute | solution.py:286
  49.9 14.8 %collective-permute-start.20 = (bf16[128,256]{0,1:T(8,128)(2,1)S(1)}, bf16[128,256]{0,1:T(8,128)(2,1)S(1)}, u32[]{:S(2)}, u32[]{:S(2)}) collective-permute-start(bf16[128,256]{0,1:T(8,128)(2,1)S(1)} %dynamic-slice_bitcast_fusion.3), channel_id=1, source_target_pairs={{0,24},{4,28},{8,16},{12,20},{16,8},{20,12},{24,0},{28,4},{1,25},{... | collective-permute-start | bytes 196616 | tf_op jit(solution)/shard_map/ppermute | solution.py:286
  64.8 12.8 %collective-permute-start.21 = (bf16[512,256]{0,1:T(8,128)(2,1)S(1)}, bf16[512,256]{0,1:T(8,128)(2,1)S(1)}, u32[]{:S(2)}, u32[]{:S(2)}) collective-permute-start(bf16[512,256]{0,1:T(8,128)(2,1)S(1)} %pad_maximum_fusion.18), channel_id=1, source_target_pairs={{0,4},{4,0},{8,12},{12,8},{16,20},{20,16},{24,28},{28,24},{1,5},{5... | collective-permute-start | bytes 786440 | tf_op jit(solution)/shard_map/ppermute | solution.py:286
  79.9 7.8 %collective-permute-start.22 = (bf16[384,1024]{1,0:T(8,128)(2,1)}, bf16[384,1024]{1,0:T(8,128)(2,1)S(1)}, u32[]{:S(2)}, u32[]{:S(2)}) collective-permute-start(bf16[384,1024]{1,0:T(8,128)(2,1)} %convolution_convert_fusion.3), channel_id=1, source_target_pairs={{0,1},{1,0},{2,3},{3,2},{4,5},{5,4},{6,7},{7,6},{8,9},{9,8},{10,11... | collective-permute-start | bytes 2359304 | tf_op jit(solution)/shard_map/ppermute | solution.py:295
  79.9 15.3 %collective-permute-start.26 = (bf16[128,1024]{1,0:T(8,128)(2,1)S(1)}, bf16[128,1024]{1,0:T(8,128)(2,1)S(1)}, u32[]{:S(2)}, u32[]{:S(2)}) collective-permute-start(bf16[128,1024]{1,0:T(8,128)(2,1)S(1)} %constant_dynamic-slice_fusion.3), channel_id=1, source_target_pairs={{0,16},{4,20},{8,24},{12,28},{16,0},{20,4},{24,8},{28,12},{1,17},{... | collective-permute-start | bytes 786440 | tf_op jit(solution)/shard_map/ppermute | solution.py:286
  80.3 20.5 %collective-permute-start.27 = (bf16[128,1024]{1,0:T(8,128)(2,1)S(1)}, bf16[128,1024]{1,0:T(8,128)(2,1)S(1)}, u32[]{:S(2)}, u32[]{:S(2)}) collective-permute-start(bf16[128,1024]{1,0:T(8,128)(2,1)S(1)} %constant_dynamic-slice_fusion.3), channel_id=1, source_target_pairs={{0,8},{4,12},{8,0},{12,4},{16,24},{20,28},{24,16},{28,20},{1,9},{5... | collective-permute-start | bytes 786440 | tf_op jit(solution)/shard_map/ppermute | solution.py:286
  82.9 17.9 %collective-permute-start.28 = (bf16[128,1024]{1,0:T(8,128)(2,1)S(1)}, bf16[128,1024]{1,0:T(8,128)(2,1)S(1)}, u32[]{:S(2)}, u32[]{:S(2)}) collective-permute-start(bf16[128,1024]{1,0:T(8,128)(2,1)S(1)} %constant_dynamic-slice_fusion.3), channel_id=1, source_target_pairs={{0,24},{4,28},{8,16},{12,20},{16,8},{20,12},{24,0},{28,4},{1,25},{... | collective-permute-start | bytes 786440 | tf_op jit(solution)/shard_map/ppermute | solution.py:286
  87.1 13.7 %collective-permute-start.30 = (bf16[192,1024]{1,0:T(8,128)(2,1)S(1)}, bf16[192,1024]{1,0:T(8,128)(2,1)S(1)}, u32[]{:S(2)}, u32[]{:S(2)}) collective-permute-start(bf16[192,1024]{1,0:T(8,128)(2,1)S(1)} %convolution_convert_fusion.7), channel_id=1, source_target_pairs={{0,2},{2,0},{1,3},{3,1},{4,6},{6,4},{5,7},{7,5},{8,10},{10,8},{9,1... | collective-permute-start | bytes 1179656 | tf_op jit(solution)/shard_map/ppermute | solution.py:292
  88.1 18.2 %collective-permute-start.23 = (bf16[192,1024]{1,0:T(8,128)(2,1)S(1)}, bf16[192,1024]{1,0:T(8,128)(2,1)S(1)}, u32[]{:S(2)}, u32[]{:S(2)}) collective-permute-start(bf16[192,1024]{1,0:T(8,128)(2,1)S(1)} %slice.853), channel_id=1, source_target_pairs={{0,2},{2,0},{1,3},{3,1},{4,6},{6,4},{5,7},{7,5},{8,10},{10,8},{9,1... | collective-permute-start | bytes 1179656 | tf_op jit(solution)/shard_map/ppermute | solution.py:292
  107.6 9.9 %collective-permute-start.24 = (bf16[192,1024]{1,0:T(8,128)(2,1)S(1)}, bf16[192,1024]{1,0:T(8,128)(2,1)S(1)}, u32[]{:S(2)}, u32[]{:S(2)}) collective-permute-start(bf16[192,1024]{1,0:T(8,128)(2,1)S(1)} %add_convert_fusion), channel_id=1, source_target_pairs={{0,2},{2,0},{1,3},{3,1},{4,6},{6,4},{5,7},{7,5},{8,10},{10,8},{9,1... | collective-permute-start | bytes 1179656 | tf_op jit(solution)/shard_map/ppermute | solution.py:292
  109.1 36.5 %collective-permute-start.31 = (bf16[384,1024]{1,0:T(8,128)(2,1)}, bf16[384,1024]{1,0:T(8,128)(2,1)}, u32[]{:S(2)}, u32[]{:S(2)}) collective-permute-start(bf16[384,1024]{1,0:T(8,128)(2,1)} %pad_maximum_fusion.8), channel_id=1, source_target_pairs={{0,1},{1,0},{2,3},{3,2},{4,5},{5,4},{6,7},{7,6},{8,9},{9,8},{10,11... | collective-permute-start | bytes 2359304 | tf_op jit(solution)/shard_map/ppermute | solution.py:295
  110.2 38.4 %collective-permute-start.29 = (bf16[512,1024]{1,0:T(8,128)(2,1)}, bf16[512,1024]{1,0:T(8,128)(2,1)}, u32[]{:S(2)}, u32[]{:S(2)}) collective-permute-start(bf16[512,1024]{1,0:T(8,128)(2,1)} %pad_maximum_fusion.4), channel_id=1, source_target_pairs={{0,4},{4,0},{8,12},{12,8},{16,20},{20,16},{24,28},{28,24},{1,5},{5... | collective-permute-start | bytes 3145736 | tf_op jit(solution)/shard_map/ppermute | solution.py:286
  118.5 30.1 %collective-permute-start.25 = (bf16[384,1024]{1,0:T(8,128)(2,1)}, bf16[384,1024]{1,0:T(8,128)(2,1)}, u32[]{:S(2)}, u32[]{:S(2)}) collective-permute-start(bf16[384,1024]{1,0:T(8,128)(2,1)} %pad_maximum_fusion.7), channel_id=1, source_target_pairs={{0,1},{1,0},{2,3},{3,2},{4,5},{5,4},{6,7},{7,6},{8,9},{9,8},{10,11... | collective-permute-start | bytes 2359304 | tf_op jit(solution)/shard_map/ppermute | solution.py:295
  118.7 22.9 %collective-permute-start.32 = (bf16[128,1024]{1,0:T(8,128)(2,1)S(1)}, bf16[128,1024]{1,0:T(8,128)(2,1)S(1)}, u32[]{:S(2)}, u32[]{:S(2)}) collective-permute-start(bf16[128,1024]{1,0:T(8,128)(2,1)S(1)} %bitcast.150), channel_id=1, source_target_pairs={{0,4},{4,0},{8,12},{12,8},{16,20},{20,16},{24,28},{28,24},{1,5},{5... | collective-permute-start | bytes 786440 | tf_op jit(solution)/shard_map/ppermute | solution.py:286
  142.6 27.1 %collective-permute-start.33 = (bf16[256,1024]{1,0:T(8,128)(2,1)S(1)}, bf16[256,1024]{1,0:T(8,128)(2,1)S(1)}, u32[]{:S(2)}, u32[]{:S(2)}) collective-permute-start(bf16[256,1024]{1,0:T(8,128)(2,1)S(1)} %pad_maximum_fusion.15.refs_0_), channel_id=1, source_target_pairs={{0,16},{4,20},{8,24},{12,28},{16,0},{20,4},{24,8},{28,12},{1,17},{... | collective-permute-start | bytes 1572872 | tf_op jit(solution)/shard_map/ppermute | solution.py:286
  143.3 26.4 %collective-permute-start.34 = (bf16[256,1024]{1,0:T(8,128)(2,1)S(1)}, bf16[256,1024]{1,0:T(8,128)(2,1)S(1)}, u32[]{:S(2)}, u32[]{:S(2)}) collective-permute-start(bf16[256,1024]{1,0:T(8,128)(2,1)S(1)} %pad_maximum_fusion.15.refs_0_), channel_id=1, source_target_pairs={{0,8},{4,12},{8,0},{12,4},{16,24},{20,28},{24,16},{28,20},{1,9},{5... | collective-permute-start | bytes 1572872 | tf_op jit(solution)/shard_map/ppermute | solution.py:286
  145.6 34.0 %collective-permute-start.35 = (bf16[256,1024]{1,0:T(8,128)(2,1)S(1)}, bf16[256,1024]{1,0:T(8,128)(2,1)S(1)}, u32[]{:S(2)}, u32[]{:S(2)}) collective-permute-start(bf16[256,1024]{1,0:T(8,128)(2,1)S(1)} %pad_maximum_fusion.15.refs_0_), channel_id=1, source_target_pairs={{0,24},{4,28},{8,16},{12,20},{16,8},{20,12},{24,0},{28,4},{1,25},{... | collective-permute-start | bytes 1572872 | tf_op jit(solution)/shard_map/ppermute | solution.py:286
  195.2 35.4 %collective-permute-start.66 = (bf16[512,1024]{1,0:T(8,128)(2,1)}, bf16[512,1024]{1,0:T(8,128)(2,1)S(1)}, u32[]{:S(2)}, u32[]{:S(2)}) collective-permute-start(bf16[512,1024]{1,0:T(8,128)(2,1)} %convolution_convert_fusion.1), channel_id=1, source_target_pairs={{0,4},{4,0},{8,12},{12,8},{16,20},{20,16},{24,28},{28,24},{1,5},{5... | collective-permute-start | bytes 3145736 | tf_op jit(solution)/shard_map/ppermute | solution.py:286
  202.5 41.1 %collective-permute-start.37 = (bf16[384,1024]{1,0:T(8,128)(2,1)S(1)}, bf16[384,1024]{1,0:T(8,128)(2,1)S(1)}, u32[]{:S(2)}, u32[]{:S(2)}) collective-permute-start(bf16[384,1024]{1,0:T(8,128)(2,1)S(1)} %convolution_convert_fusion.4), channel_id=1, source_target_pairs={{0,1},{1,0},{2,3},{3,2},{4,5},{5,4},{6,7},{7,6},{8,9},{9,8},{10,11... | collective-permute-start | bytes 2359304 | tf_op jit(solution)/shard_map/ppermute | solution.py:295
  202.8 11.3 %collective-permute-start.39 = (bf16[192,1024]{1,0:T(8,128)(2,1)S(1)}, bf16[192,1024]{1,0:T(8,128)(2,1)S(1)}, u32[]{:S(2)}, u32[]{:S(2)}) collective-permute-start(bf16[192,1024]{1,0:T(8,128)(2,1)S(1)} %slice.851), channel_id=1, source_target_pairs={{0,2},{2,0},{1,3},{3,1},{4,6},{6,4},{5,7},{7,5},{8,10},{10,8},{9,1... | collective-permute-start | bytes 1179656 | tf_op jit(solution)/shard_map/ppermute | solution.py:292
  216.4 10.5 %collective-permute-start.40 = (bf16[192,1024]{1,0:T(8,128)(2,1)S(1)}, bf16[192,1024]{1,0:T(8,128)(2,1)S(1)}, u32[]{:S(2)}, u32[]{:S(2)}) collective-permute-start(bf16[192,1024]{1,0:T(8,128)(2,1)S(1)} %multiply_convert_fusion.2), channel_id=1, source_target_pairs={{0,2},{2,0},{1,3},{3,1},{4,6},{6,4},{5,7},{7,5},{8,10},{10,8},{9,1... | collective-permute-start | bytes 1179656 | tf_op jit(solution)/shard_map/ppermute | solution.py:292
  227.0 19.9 %collective-permute-start.41 = (bf16[384,1024]{1,0:T(8,128)(2,1)S(1)}, bf16[384,1024]{1,0:T(8,128)(2,1)S(1)}, u32[]{:S(2)}, u32[]{:S(2)}) collective-permute-start(bf16[384,1024]{1,0:T(8,128)(2,1)S(1)} %pad_maximum_fusion.9), channel_id=1, source_target_pairs={{0,1},{1,0},{2,3},{3,2},{4,5},{5,4},{6,7},{7,6},{8,9},{9,8},{10,11... | collective-permute-start | bytes 2359304 | tf_op jit(solution)/shard_map/ppermute | solution.py:295
  229.1 36.5 %collective-permute-start.62 = (bf16[512,1024]{1,0:T(8,128)(2,1)}, bf16[512,1024]{1,0:T(8,128)(2,1)}, u32[]{:S(2)}, u32[]{:S(2)}) collective-permute-start(bf16[512,1024]{1,0:T(8,128)(2,1)} %convolution_convert_fusion), channel_id=1, source_target_pairs={{0,4},{4,0},{8,12},{12,8},{16,20},{20,16},{24,28},{28,24},{1,5},{5... | collective-permute-start | bytes 3145736 | tf_op jit(solution)/shard_map/ppermute | solution.py:286
  231.8 73.1 %collective-permute-start.67 = (bf16[128,1024]{1,0:T(8,128)(2,1)}, bf16[128,1024]{1,0:T(8,128)(2,1)}, u32[]{:S(2)}, u32[]{:S(2)}) collective-permute-start(bf16[128,1024]{1,0:T(8,128)(2,1)} %get-tuple-element.147), channel_id=1, source_target_pairs={{0,16},{4,20},{8,24},{12,28},{16,0},{20,4},{24,8},{28,12},{1,17},{... | collective-permute-start | bytes 786440 | tf_op jit(solution)/shard_map/ppermute | solution.py:286
  245.5 19.3 %collective-permute-start.38 = (bf16[192,1024]{1,0:T(8,128)(2,1)}, bf16[192,1024]{1,0:T(8,128)(2,1)}, u32[]{:S(2)}, u32[]{:S(2)}) collective-permute-start(bf16[192,1024]{1,0:T(8,128)(2,1)} %slice.852), channel_id=1, source_target_pairs={{0,2},{2,0},{1,3},{3,1},{4,6},{6,4},{5,7},{7,5},{8,10},{10,8},{9,1... | collective-permute-start | bytes 1179656 | tf_op jit(solution)/shard_map/ppermute | solution.py:292
  264.7 25.8 %collective-permute-start.45 = (bf16[384,1024]{1,0:T(8,128)(2,1)S(1)}, bf16[384,1024]{1,0:T(8,128)(2,1)S(1)}, u32[]{:S(2)}, u32[]{:S(2)}) collective-permute-start(bf16[384,1024]{1,0:T(8,128)(2,1)S(1)} %get-tuple-element.160), channel_id=1, source_target_pairs={{0,1},{1,0},{2,3},{3,2},{4,5},{5,4},{6,7},{7,6},{8,9},{9,8},{10,11... | collective-permute-start | bytes 2359304 | tf_op jit(solution)/shard_map/ppermute | solution.py:295
  267.0 16.3 %collective-permute-start.63 = (bf16[128,1024]{1,0:T(8,128)(2,1)S(1)}, bf16[128,1024]{1,0:T(8,128)(2,1)S(1)}, u32[]{:S(2)}, u32[]{:S(2)}) collective-permute-start(bf16[128,1024]{1,0:T(8,128)(2,1)S(1)} %get-tuple-element.150), channel_id=1, source_target_pairs={{0,16},{4,20},{8,24},{12,28},{16,0},{20,4},{24,8},{28,12},{1,17},{... | collective-permute-start | bytes 786440 | tf_op jit(solution)/shard_map/ppermute | solution.py:286
  268.3 18.5 %collective-permute-start.64 = (bf16[128,1024]{1,0:T(8,128)(2,1)S(1)}, bf16[128,1024]{1,0:T(8,128)(2,1)S(1)}, u32[]{:S(2)}, u32[]{:S(2)}) collective-permute-start(bf16[128,1024]{1,0:T(8,128)(2,1)S(1)} %get-tuple-element.149), channel_id=1, source_target_pairs={{0,8},{4,12},{8,0},{12,4},{16,24},{20,28},{24,16},{28,20},{1,9},{5... | collective-permute-start | bytes 786440 | tf_op jit(solution)/shard_map/ppermute | solution.py:286
  269.9 19.1 %collective-permute-start.65 = (bf16[128,1024]{1,0:T(8,128)(2,1)S(1)}, bf16[128,1024]{1,0:T(8,128)(2,1)S(1)}, u32[]{:S(2)}, u32[]{:S(2)}) collective-permute-start(bf16[128,1024]{1,0:T(8,128)(2,1)S(1)} %get-tuple-element.148), channel_id=1, source_target_pairs={{0,24},{4,28},{8,16},{12,20},{16,8},{20,12},{24,0},{28,4},{1,25},{... | collective-permute-start | bytes 786440 | tf_op jit(solution)/shard_map/ppermute | solution.py:286
  283.4 23.2 %collective-permute-start.68 = (bf16[128,1024]{1,0:T(8,128)(2,1)}, bf16[128,1024]{1,0:T(8,128)(2,1)}, u32[]{:S(2)}, u32[]{:S(2)}) collective-permute-start(bf16[128,1024]{1,0:T(8,128)(2,1)} %get-tuple-element.146), channel_id=1, source_target_pairs={{0,8},{4,12},{8,0},{12,4},{16,24},{20,28},{24,16},{28,20},{1,9},{5... | collective-permute-start | bytes 786440 | tf_op jit(solution)/shard_map/ppermute | solution.py:286
  286.8 24.5 %collective-permute-start.69 = (bf16[128,1024]{1,0:T(8,128)(2,1)}, bf16[128,1024]{1,0:T(8,128)(2,1)}, u32[]{:S(2)}, u32[]{:S(2)}) collective-permute-start(bf16[128,1024]{1,0:T(8,128)(2,1)} %get-tuple-element.145), channel_id=1, source_target_pairs={{0,24},{4,28},{8,16},{12,20},{16,8},{20,12},{24,0},{28,4},{1,25},{... | collective-permute-start | bytes 786440 | tf_op jit(solution)/shard_map/ppermute | solution.py:286
  289.0 57.3 %collective-permute-start.57 = (bf16[512,1024]{1,0:T(8,128)(2,1)}, bf16[512,1024]{1,0:T(8,128)(2,1)}, u32[]{:S(2)}, u32[]{:S(2)}) collective-permute-start(bf16[512,1024]{1,0:T(8,128)(2,1)} %pad_maximum_fusion.5), channel_id=1, source_target_pairs={{0,4},{4,0},{8,12},{12,8},{16,20},{20,16},{24,28},{28,24},{1,5},{5... | collective-permute-start | bytes 3145736 | tf_op jit(solution)/shard_map/ppermute | solution.py:286
  296.9 4.3 %collective-permute-start.43 = (f32[5632]{0:T(1024)S(1)}, f32[5632]{0:T(1024)S(1)}, u32[]{:S(2)}, u32[]{:S(2)}) collective-permute-start(f32[5632]{0:T(1024)S(1)} %pad_maximum_fusion.24), channel_id=1, source_target_pairs={{0,2},{2,0},{1,3},{3,1},{4,6},{6,4},{5,7},{7,5},{8,10},{10,8},{9,1... | collective-permute-start | bytes 67592 | tf_op jit(solution)/shard_map/ppermute | solution.py:292
  301.3 53.7 %collective-permute-start.46 = (bf16[192,1024]{1,0:T(8,128)(2,1)}, bf16[192,1024]{1,0:T(8,128)(2,1)}, u32[]{:S(2)}, u32[]{:S(2)}) collective-permute-start(bf16[192,1024]{1,0:T(8,128)(2,1)} %slice.850), channel_id=1, source_target_pairs={{0,2},{2,0},{1,3},{3,1},{4,6},{6,4},{5,7},{7,5},{8,10},{10,8},{9,1... | collective-permute-start | bytes 1179656 | tf_op jit(solution)/shard_map/ppermute | solution.py:292
  304.8 12.1 %collective-permute-start.50 = (f32[1,7168]{1,0:T(1,128)S(1)}, f32[1,7168]{1,0:T(1,128)S(1)}, u32[]{:S(2)}, u32[]{:S(2)}) collective-permute-start(f32[1,7168]{1,0:T(1,128)S(1)} %bitcast.157), channel_id=1, source_target_pairs={{0,24},{4,28},{8,16},{12,20},{16,8},{20,12},{24,0},{28,4},{1,25},{... | collective-permute-start | bytes 86024 | tf_op jit(solution)/shard_map/ppermute | solution.py:286
  306.5 10.4 %collective-permute-start.49 = (f32[1,7168]{1,0:T(1,128)S(1)}, f32[1,7168]{1,0:T(1,128)S(1)}, u32[]{:S(2)}, u32[]{:S(2)}) collective-permute-start(f32[1,7168]{1,0:T(1,128)S(1)} %bitcast.158), channel_id=1, source_target_pairs={{0,8},{4,12},{8,0},{12,4},{16,24},{20,28},{24,16},{28,20},{1,9},{5... | collective-permute-start | bytes 86024 | tf_op jit(solution)/shard_map/ppermute | solution.py:286
  311.3 6.8 %collective-permute-start.48 = (f32[1,7168]{1,0:T(1,128)S(1)}, f32[1,7168]{1,0:T(1,128)S(1)}, u32[]{:S(2)}, u32[]{:S(2)}) collective-permute-start(f32[1,7168]{1,0:T(1,128)S(1)} %bitcast.159), channel_id=1, source_target_pairs={{0,16},{4,20},{8,24},{12,28},{16,0},{20,4},{24,8},{28,12},{1,17},{... | collective-permute-start | bytes 86024 | tf_op jit(solution)/shard_map/ppermute | solution.py:286
  316.9 58.8 %collective-permute-start.44 = (f32[1,192,1024]{2,1,0:T(8,128)}, f32[1,192,1024]{2,1,0:T(8,128)}, u32[]{:S(2)}, u32[]{:S(2)}) collective-permute-start(f32[1,192,1024]{2,1,0:T(8,128)} %get-tuple-element.196), channel_id=1, source_target_pairs={{0,1},{1,0},{2,3},{3,2},{4,5},{5,4},{6,7},{7,6},{8,9},{9,8},{10,11... | collective-permute-start | bytes 2359304 | tf_op jit(solution)/shard_map/ppermute | solution.py:295
  317.0 33.1 %collective-permute-start.70 = (bf16[64,2048]{1,0:T(8,128)(2,1)}, bf16[64,2048]{1,0:T(8,128)(2,1)S(1)}, u32[]{:S(2)}, u32[]{:S(2)}) collective-permute-start(bf16[64,2048]{1,0:T(8,128)(2,1)} %fusion.62), channel_id=1, source_target_pairs={{0,2},{2,0},{1,3},{3,1},{4,6},{6,4},{5,7},{7,5},{8,10},{10,8},{9,1... | collective-permute-start | bytes 786440 | tf_op jit(solution)/shard_map/ppermute | solution.py:292
  318.2 5.3 %collective-permute-start.51 = (f32[4,7168]{1,0:T(4,128)S(1)}, f32[4,7168]{1,0:T(4,128)S(1)}, u32[]{:S(2)}, u32[]{:S(2)}) collective-permute-start(f32[4,7168]{1,0:T(4,128)S(1)} %pad_maximum_fusion.22), channel_id=1, source_target_pairs={{0,4},{4,0},{8,12},{12,8},{16,20},{20,16},{24,28},{28,24},{1,5},{5... | collective-permute-start | bytes 344072 | tf_op jit(solution)/shard_map/ppermute | solution.py:286
  324.0 4.2 %collective-permute-start.52 = (f32[2048]{0:T(1024)S(1)}, f32[2048]{0:T(1024)S(1)}, u32[]{:S(2)}, u32[]{:S(2)}) collective-permute-start(f32[2048]{0:T(1024)S(1)} %pad_maximum_fusion.27), channel_id=1, source_target_pairs={{0,1},{1,0},{2,3},{3,2},{4,5},{5,4},{6,7},{7,6},{8,9},{9,8},{10,11... | collective-permute-start | bytes 24584 | tf_op jit(solution)/shard_map/ppermute | solution.py:295
  331.9 4.8 %collective-permute-start.54 = (f32[1,2,128]{2,0,1:T(1,128)S(1)}, f32[1,2,128]{2,0,1:T(1,128)S(1)}, u32[]{:S(2)}, u32[]{:S(2)}) collective-permute-start(f32[1,2,128]{2,0,1:T(1,128)S(1)} %get-tuple-element.186), channel_id=1, source_target_pairs={{0,16},{4,20},{8,24},{12,28},{16,0},{20,4},{24,8},{28,12},{1,17},{... | collective-permute-start | bytes 3080 | tf_op jit(solution)/shard_map/ppermute | solution.py:286
  340.2 5.4 %collective-permute-start.56 = (f32[1,2,128]{2,0,1:T(1,128)S(1)}, f32[1,2,128]{2,0,1:T(1,128)S(1)}, u32[]{:S(2)}, u32[]{:S(2)}) collective-permute-start(f32[1,2,128]{2,0,1:T(1,128)S(1)} %get-tuple-element.184), channel_id=1, source_target_pairs={{0,24},{4,28},{8,16},{12,20},{16,8},{20,12},{24,0},{28,4},{1,25},{... | collective-permute-start | bytes 3080 | tf_op jit(solution)/shard_map/ppermute | solution.py:286
  348.0 13.2 %collective-permute-start.60 = (bf16[128,1024]{1,0:T(8,128)(2,1)S(1)}, bf16[128,1024]{1,0:T(8,128)(2,1)S(1)}, u32[]{:S(2)}, u32[]{:S(2)}) collective-permute-start(bf16[128,1024]{1,0:T(8,128)(2,1)S(1)} %get-tuple-element.152), channel_id=1, source_target_pairs={{0,24},{4,28},{8,16},{12,20},{16,8},{20,12},{24,0},{28,4},{1,25},{... | collective-permute-start | bytes 786440 | tf_op jit(solution)/shard_map/ppermute | solution.py:286
  350.1 11.7 %collective-permute-start.59 = (bf16[128,1024]{1,0:T(8,128)(2,1)S(1)}, bf16[128,1024]{1,0:T(8,128)(2,1)S(1)}, u32[]{:S(2)}, u32[]{:S(2)}) collective-permute-start(bf16[128,1024]{1,0:T(8,128)(2,1)S(1)} %get-tuple-element.153), channel_id=1, source_target_pairs={{0,8},{4,12},{8,0},{12,4},{16,24},{20,28},{24,16},{28,20},{1,9},{5... | collective-permute-start | bytes 786440 | tf_op jit(solution)/shard_map/ppermute | solution.py:286
  350.8 17.8 %collective-permute-start.58 = (bf16[128,1024]{1,0:T(8,128)(2,1)S(1)}, bf16[128,1024]{1,0:T(8,128)(2,1)S(1)}, u32[]{:S(2)}, u32[]{:S(2)}) collective-permute-start(bf16[128,1024]{1,0:T(8,128)(2,1)S(1)} %get-tuple-element.151), channel_id=1, source_target_pairs={{0,16},{4,20},{8,24},{12,28},{16,0},{20,4},{24,8},{28,12},{1,17},{... | collective-permute-start | bytes 786440 | tf_op jit(solution)/shard_map/ppermute | solution.py:286
  361.1 15.9 %collective-permute-start.47 = (f32[1,192,1024]{2,1,0:T(8,128)S(1)}, f32[1,192,1024]{2,1,0:T(8,128)S(1)}, u32[]{:S(2)}, u32[]{:S(2)}) collective-permute-start(f32[1,192,1024]{2,1,0:T(8,128)S(1)} %get-tuple-element.198), channel_id=1, source_target_pairs={{0,1},{1,0},{2,3},{3,2},{4,5},{5,4},{6,7},{7,6},{8,9},{9,8},{10,11... | collective-permute-start | bytes 2359304 | tf_op jit(solution)/shard_map/ppermute | solution.py:295
  369.9 5.0 %collective-permute-start.61 = (bf16[64,1024]{1,0:T(8,128)(2,1)S(1)}, bf16[64,1024]{1,0:T(8,128)(2,1)S(1)}, u32[]{:S(2)}, u32[]{:S(2)}) collective-permute-start(bf16[64,1024]{1,0:T(8,128)(2,1)S(1)} %dynamic-slice_convert_fusion), channel_id=1, source_target_pairs={{0,2},{2,0},{1,3},{3,1},{4,6},{6,4},{5,7},{7,5},{8,10},{10,8},{9,1... | collective-permute-start | bytes 393224 | tf_op jit(solution)/shard_map/ppermute | solution.py:292
  (121 other events, 1370.1 us)
